TPU v7x, 128 devices: a whole 4x4x4 slice. The times are simulated.
128 devices in a mesh: ctx: 16 (over y, x), exp: 8 (over z, core).
Axes of the slice: x: 4, y: 4, z: 4, core: 2. Of those that a mesh axis runs over, the one named last changes fastest.
Arguments:
- queries: bfloat16 [8192, 4096], P(('ctx', 'exp')), may hold values from -6 to 6
- rotated_key_heads: bfloat16 [8192, 512], P(('ctx', 'exp')), may hold values from -15 to 15
- stacked_value_heads: bfloat16 [8192, 512], P(('ctx', 'exp')), may hold values from -6 to 6
- moe_rows: bfloat16 [16384, 4096], P(('ctx', 'exp')), may hold values from -6 to 6
- expert_ids: int32 [16384, 8], P(('ctx', 'exp')), may hold values from 0 to 127, all different within a row; in each aligned block of 128 rows (0 to 127, 128 to 255, ...) at most 10 rows name the same one
- route_weights: float32 [16384, 8], P(('ctx', 'exp')), may hold values from 0.05 to 0.35
- w_gate: bfloat16 [128, 4096, 768], P(('ctx', 'exp')), may hold values from -0.09375 to 0.09375
- w_up: bfloat16 [128, 4096, 768], P(('ctx', 'exp')), may hold values from -0.09375 to 0.09375
- w_down: bfloat16 [128, 768, 4096], P(('ctx', 'exp')), may hold values from -0.21875 to 0.21875
Outputs:
- attended: bfloat16 [8192, 4096], P(('ctx', 'exp'))
- expert_mix: bfloat16 [16384, 4096], P(('ctx', 'exp'))
Inputs may be any that keep to these rules, and one draw needn't show every extreme that they name: `expert_ids`: the 8 ids of a token are distinct. In each aligned block of 128 rows (the rows of one device) no expert is named by more than 10 rows, a bound that some block reaches.
All inputs are finite; a program needn't handle non-finite values.
Results may differ from a plain program's by a relative error of at most 0.0058.
Values may be sent and summed in bfloat16 or wider, within the bound.
A program may use at most 192 MiB of HBM per device.

v0:
```python
import math

import jax
import jax.numpy as jnp
from jax import lax
from jax.sharding import PartitionSpec as P

D = 4096
QUERY_HEADS = 32
KEY_VALUE_HEADS = 4
HEAD_WIDTH = 128
TOPK = 8


def attend(queries, rotated_key_heads, stacked_value_heads):
    context_count = lax.axis_size("ctx")
    exp_count = lax.axis_size("exp")
    sequence_rows = queries.shape[0]
    heads_here = QUERY_HEADS // context_count
    repeat_factor = context_count // KEY_VALUE_HEADS
    key_dispersion = jnp.repeat(
        rotated_key_heads.reshape(sequence_rows, KEY_VALUE_HEADS, HEAD_WIDTH), repeat_factor, axis=1
    ).reshape(sequence_rows, context_count * HEAD_WIDTH)
    value_dispersion = jnp.repeat(
        stacked_value_heads.reshape(sequence_rows, KEY_VALUE_HEADS, HEAD_WIDTH),
        repeat_factor,
        axis=1,
    ).reshape(sequence_rows, context_count * HEAD_WIDTH)
    local_query, local_key, local_value = (
        lax.all_to_all(queries, "ctx", split_axis=1, concat_axis=0, tiled=True),
        lax.all_to_all(key_dispersion, "ctx", split_axis=1, concat_axis=0, tiled=True),
        lax.all_to_all(value_dispersion, "ctx", split_axis=1, concat_axis=0, tiled=True),
    )
    query_count = local_query.shape[0]
    row_ids = jnp.arange(query_count, dtype=jnp.int32)
    exp_here = lax.axis_index("exp")
    query_pos = (
        row_ids // sequence_rows * exp_count + exp_here
    ) * sequence_rows + row_ids % sequence_rows
    query_grid = local_query.reshape(query_count, heads_here, HEAD_WIDTH)
    scale_factor = 1.0 / math.sqrt(HEAD_WIDTH)

    def block_step(state, key_block, value_block, key_pos):
        row_max, row_sum, accum = state
        scores = (
            jnp.einsum("qhd,kd->hqk", query_grid, key_block, preferred_element_type=jnp.float32)
            * scale_factor
        )
        allowed = key_pos[None, None, :] <= query_pos[None, :, None]
        scores = jnp.where(allowed, scores, -1e30)
        new_max = jnp.maximum(row_max, jnp.max(scores, axis=2))
        probs = jnp.where(allowed, jnp.exp(scores - new_max[:, :, None]), 0.0).astype(jnp.bfloat16)
        factor = jnp.exp(row_max - new_max)
        row_sum = row_sum * factor + jnp.sum(probs.astype(jnp.float32), axis=2)
        accum = accum * factor.T[:, :, None] + jnp.einsum(
            "hqk,kd->qhd", probs, value_block, preferred_element_type=jnp.float32
        )
        return (new_max, row_sum, accum)

    initial = (
        jnp.full((heads_here, query_count), -1e30, jnp.float32),
        jnp.zeros((heads_here, query_count), jnp.float32),
        jnp.zeros((query_count, heads_here, HEAD_WIDTH), jnp.float32),
    )
    state = initial
    key_piece = lax.all_gather(local_key, "exp", axis=0, tiled=True)
    value_piece = lax.all_gather(local_value, "exp", axis=0, tiled=True)
    count = key_piece.shape[0]
    global_ids = jnp.arange(count, dtype=jnp.int32)
    source_exp = global_ids // query_count
    within = global_ids % query_count
    key_pos = (
        within // sequence_rows * exp_count + source_exp
    ) * sequence_rows + within % sequence_rows
    block_rows = 1024
    whole = count // block_rows * block_rows

    def scan_step(inner, parts):
        return (block_step(inner, parts[0], parts[1], parts[2]), 0)

    state = lax.scan(
        scan_step,
        state,
        (
            key_piece.reshape(whole // block_rows, block_rows, HEAD_WIDTH),
            value_piece.reshape(whole // block_rows, block_rows, HEAD_WIDTH),
            key_pos.reshape(whole // block_rows, block_rows),
        ),
    )[0]
    row_max, row_sum, accum = state
    head_out = (
        (accum / row_sum.T[:, :, None])
        .astype(jnp.bfloat16)
        .reshape(query_count, heads_here * HEAD_WIDTH)
    )
    return lax.all_to_all(head_out, "ctx", split_axis=0, concat_axis=1, tiled=True)


def expert_ffn(rows, w_gate, w_up, w_down):
    gate_in = jnp.dot(rows, w_gate[0], preferred_element_type=jnp.float32)
    up_in = jnp.dot(rows, w_up[0], preferred_element_type=jnp.float32)
    hidden = (jax.nn.silu(gate_in) * up_in).astype(jnp.bfloat16)
    return jnp.dot(hidden, w_down[0], preferred_element_type=jnp.float32).astype(jnp.bfloat16)


def run_live(received, live_mask, w_gate, w_up, w_down):
    flat_rows = received.reshape(-1, D)
    row_total = flat_rows.shape[0]
    live_flat = live_mask.reshape(row_total)
    order_pos = jnp.cumsum(live_flat) - live_flat
    block_rows = min(256, row_total)
    span = -(-row_total // block_rows) * block_rows
    compact = (
        jnp.full((span,), row_total, jnp.int32)
        .at[jnp.where(live_flat > 0, order_pos, span)]
        .set(jnp.arange(row_total, dtype=jnp.int32), mode="drop")
    )
    with_blank = jnp.concatenate([flat_rows, jnp.zeros((1, D), flat_rows.dtype)], 0)
    live_total = jnp.sum(live_flat)
    block_count = (live_total + block_rows - 1) // block_rows

    def one_block(index, output):
        picked = lax.dynamic_slice_in_dim(compact, index * block_rows, block_rows)
        return output.at[picked].set(expert_ffn(with_blank[picked], w_gate, w_up, w_down))

    output = lax.fori_loop(0, block_count, one_block, jnp.zeros((row_total + 1, D), jnp.bfloat16))
    return output[:row_total].reshape(received.shape)


def mixture(moe_rows, expert_ids, route_weights, w_gate, w_up, w_down):
    context_count = lax.axis_size("ctx")
    exp_count = lax.axis_size("exp")
    experts = context_count * exp_count
    token_count = moe_rows.shape[0]
    pair_count = token_count * TOPK
    capacity = max(2, pair_count * 5 // (4 * experts))
    flat_ids = expert_ids.reshape(pair_count)
    one_hot = (flat_ids[:, None] == jnp.arange(experts, dtype=jnp.int32)[None, :]).astype(jnp.int32)
    earlier = jnp.cumsum(one_hot, axis=0) - one_hot
    slot_index = jnp.sum(earlier * one_hot, axis=1)
    target = flat_ids * capacity + slot_index
    filler = (
        jnp.full((experts * capacity,), pair_count, jnp.int32)
        .at[target]
        .set(jnp.arange(pair_count, dtype=jnp.int32))
    )
    padded_rows = jnp.concatenate([moe_rows, jnp.zeros((1, D), moe_rows.dtype)], 0)
    outgoing = padded_rows[filler // TOPK].reshape(experts, capacity, D)
    occupied = (filler < pair_count).astype(jnp.int32).reshape(experts, capacity)
    payload = (outgoing, occupied)
    served = run_live(
        lax.all_to_all(payload[0], ("ctx", "exp"), split_axis=0, concat_axis=0, tiled=True),
        lax.all_to_all(payload[1], ("ctx", "exp"), split_axis=0, concat_axis=0, tiled=True),
        w_gate,
        w_up,
        w_down,
    )
    returned = lax.all_to_all(served, ("ctx", "exp"), split_axis=0, concat_axis=0, tiled=True)
    gathered = returned.reshape(experts * capacity, D)[target].reshape(token_count, TOPK, D)
    mixed = jnp.zeros((token_count, D), jnp.float32)
    for slot in range(TOPK):
        mixed = mixed + route_weights[:, slot : slot + 1] * gathered[:, slot, :].astype(jnp.float32)
    return mixed.astype(jnp.bfloat16)


def body(
    queries,
    rotated_key_heads,
    stacked_value_heads,
    moe_rows,
    expert_ids,
    route_weights,
    w_gate,
    w_up,
    w_down,
):
    attended = attend(queries, rotated_key_heads, stacked_value_heads)
    expert_mix = mixture(moe_rows, expert_ids, route_weights, w_gate, w_up, w_down)
    return (attended, expert_mix)


def solution(mesh):
    placed = (
        P(("ctx", "exp"), None),
        P(("ctx", "exp"), None),
        P(("ctx", "exp"), None),
        P(("ctx", "exp"), None),
        P(("ctx", "exp"), None),
        P(("ctx", "exp"), None),
        P(("ctx", "exp"), None, None),
        P(("ctx", "exp"), None, None),
        P(("ctx", "exp"), None, None),
    )
    return jax.shard_map(
        body,
        mesh=mesh,
        in_specs=placed,
        out_specs=(P(("ctx", "exp"), None), P(("ctx", "exp"), None)),
        check_vma=False,
    )
```

profile of v0, /device:TPU:66, one launch (start us, length us, event | category | flops | bytes accessed | tf_op | source)
XLA Modules:
  0.0 951.4 jit_solution(7044856124159872539)
XLA Ops:
  8.1 14.7 %all_to_all.97 = bf16[64,16,128]{2,0,1:T(8,128)(2,1)} all-to-all(bf16[64,16,128]{2,0,1:T(8,128)(2,1)S(1)} %bitcast.185), channel_id=1, replica_groups=mesh['ctx'=16,'exp'=8] {'ctx'}, dimensions={1} | all-to-all | bytes 524288 | tf_op jit(solution)/shard_map/all_to_all | solution.py:32
  23.8 12.0 %all_to_all.98 = bf16[64,16,128]{2,0,1:T(8,128)(2,1)} all-to-all(bf16[64,16,128]{2,0,1:T(8,128)(2,1)S(1)} %bitcast.186), channel_id=1, replica_groups=mesh['ctx'=16,'exp'=8] {'ctx'}, dimensions={1} | all-to-all | bytes 524288 | tf_op jit(solution)/shard_map/all_to_all | solution.py:31
  42.9 7.0 all-to-all-start.4
  50.1 8.4 gather_fusion.1
  58.5 15.7 %reshape.242 = bf16[128,10,4096]{2,1,0:T(8,128)(2,1)} reshape(bf16[1280,4096]{1,0:T(8,128)(2,1)} %gather_fusion.1) | data formatting | bytes 20971520 | tf_op jit(solution)/shard_map/reshape | solution.py:148
  75.0 7.4 all-to-all-start.1
  92.9 25.7 %all-to-all-start.5 = ((bf16[128,10,4096]{2,1,0:T(8,128)(2,1)}), bf16[128,10,4096]{2,1,0:T(8,128)(2,1)}, u32[]{:S(2)}, u32[]{:S(2)}) async-start(bf16[128,10,4096]{2,1,0:T(8,128)(2,1)} %reshape.242), calls=%async_computation.5 | async-start | bytes 33554432 | tf_op jit(solution)/shard_map/all_to_all | solution.py:152
  118.8 118.9 %while.26 = (s32[]{:T(128)}, f32[2,1024]{1,0:T(2,128)S(1)}, f32[2,1024]{1,0:T(2,128)S(1)}, f32[1024,2,128]{0,2,1:T(8,128)S(1)}, s32[8,1024]{1,0:T(8,128)S(1)}, /...) while((s32[]{:T(128)}, f32[2,1024]{1,0:T(2,128)S(1)}, ...), condition=%wide.region_3.4_spmd.clone, body=%wide.region_0.3_spmd.clone.sunk | while | flops 1107062784 | bytes 66213016 | solution.py:81
  119.5 5.9 fusion.107
  134.4 5.9 fusion.107
  149.3 5.9 fusion.107
  164.1 5.9 fusion.107
  179.0 5.9 fusion.107
  193.9 5.9 fusion.107
  208.7 5.9 fusion.107
  223.6 5.9 fusion.107
  239.4 109.9 %all-to-all-done.5 = bf16[128,10,4096]{2,1,0:T(8,128)(2,1)} async-done(((bf16[128,10,4096]{2,1,0:T(8,128)(2,1)}), bf16[128,10,4096]{2,1,0:T(8,128)(2,1)}, u32[]{:S(2)}, u32[]{:S(2)}) %all-to-all-start.5) | async-done | bytes 10485792 | tf_op jit(solution)/shard_map/all_to_all | solution.py:152
  349.3 6.6 all-to-all-start.3
  355.9 16.5 %reshape.243 = bf16[1280,4096]{1,0:T(8,128)(2,1)} reshape(bf16[128,10,4096]{2,1,0:T(8,128)(2,1)} %all-to-all-done.5) | data formatting | bytes 20971520 | tf_op jit(solution)/shard_map/reshape | solution.py:107
  372.4 9.9 %concatenate.7 = bf16[1281,4096]{1,0:T(8,128)(2,1)} pad(bf16[1280,4096]{1,0:T(8,128)(2,1)} %reshape.243, bf16[]{:T(256)} %constant.165.clone.1), padding=0_1x0_0 | pad | bytes 20979714 | tf_op jit(solution)/shard_map/concatenate | solution.py:118
  387.5 188.9 %while.25 = (s32[]{:T(128)}, bf16[1281,4096]{1,0:T(8,128)(2,1)}, s32[]{:T(128)}, s32[1280]{0:T(1024)S(1)}, bf16[1281,4096]{1,0:T(8,128)(2,1)}, /*index=5*/bf16[1...) while((s32[]{:T(128)}, bf16[1281,4096]{1,0:T(8,128)(2,1)}, ...), condition=%wide.region_14.15_spmd, body=%wide.region_12.14_spmd.sunk | while | flops 4834068480 | bytes 45622464 | solution.py:126
  387.6 9.2 gather_fusion
  396.9 5.3 fusion.102
  402.2 9.8 %fusion.103 = bf16[256,4096]{1,0:T(8,128)(2,1)S(1)} fusion(bf16[1,768,4096]{2,1,0:T(8,128)(2,1)} %get-tuple-element.389, bf16[256,4096]{1,0:T(8,128)(2,1)} %copy-done.3, bf16[1,4096,768]{2,1,0:T(8,128)(2,1)} %get-tuple-element.388, f32[256,768]{1,0:T(8,128)S(1)} %fusion.102), kind=kOutput, calls=%fused_computation.13.clone.1 | convolution fusion | flops 3223453696 | bytes 17563648 | tf_op jit(solution)/shard_map/while/body/dot_general | solution.py:103
  411.9 13.3 %scatter_fusion = bf16[1281,4096]{1,0:T(8,128)(2,1)} fusion(bf16[1281,4096]{1,0:T(8,128)(2,1)} %get-tuple-element.371, s32[256]{0:T(256)S(1)} %compare_select_fusion.6, bf16[256,4096]{1,0:T(8,128)(2,1)S(1)} %fusion.103), kind=kCustom, calls=%fused_computation.3.clone.1 | custom fusion | bytes 6292480 | tf_op jit(solution)/shard_map/while/body/scatter | solution.py:124
  425.4 9.2 gather_fusion
  434.6 5.3 fusion.102
  440.0 9.8 %fusion.103 = bf16[256,4096]{1,0:T(8,128)(2,1)S(1)} fusion(bf16[1,768,4096]{2,1,0:T(8,128)(2,1)} %get-tuple-element.389, bf16[256,4096]{1,0:T(8,128)(2,1)} %copy-done.3, bf16[1,4096,768]{2,1,0:T(8,128)(2,1)} %get-tuple-element.388, f32[256,768]{1,0:T(8,128)S(1)} %fusion.102), kind=kOutput, calls=%fused_computation.13.clone.1 | convolution fusion | flops 3223453696 | bytes 17563648 | tf_op jit(solution)/shard_map/while/body/dot_general | solution.py:103
  449.7 13.3 %scatter_fusion = bf16[1281,4096]{1,0:T(8,128)(2,1)} fusion(bf16[1281,4096]{1,0:T(8,128)(2,1)} %get-tuple-element.371, s32[256]{0:T(256)S(1)} %compare_select_fusion.6, bf16[256,4096]{1,0:T(8,128)(2,1)S(1)} %fusion.103), kind=kCustom, calls=%fused_computation.3.clone.1 | custom fusion | bytes 6292480 | tf_op jit(solution)/shard_map/while/body/scatter | solution.py:124
  463.2 9.2 gather_fusion
  472.4 5.3 fusion.102
  477.8 9.8 %fusion.103 = bf16[256,4096]{1,0:T(8,128)(2,1)S(1)} fusion(bf16[1,768,4096]{2,1,0:T(8,128)(2,1)} %get-tuple-element.389, bf16[256,4096]{1,0:T(8,128)(2,1)} %copy-done.3, bf16[1,4096,768]{2,1,0:T(8,128)(2,1)} %get-tuple-element.388, f32[256,768]{1,0:T(8,128)S(1)} %fusion.102), kind=kOutput, calls=%fused_computation.13.clone.1 | convolution fusion | flops 3223453696 | bytes 17563648 | tf_op jit(solution)/shard_map/while/body/dot_general | solution.py:103
  487.5 13.3 %scatter_fusion = bf16[1281,4096]{1,0:T(8,128)(2,1)} fusion(bf16[1281,4096]{1,0:T(8,128)(2,1)} %get-tuple-element.371, s32[256]{0:T(256)S(1)} %compare_select_fusion.6, bf16[256,4096]{1,0:T(8,128)(2,1)S(1)} %fusion.103), kind=kCustom, calls=%fused_computation.3.clone.1 | custom fusion | bytes 6292480 | tf_op jit(solution)/shard_map/while/body/scatter | solution.py:124
  500.9 9.2 gather_fusion
  510.2 5.3 fusion.102
  515.5 9.8 %fusion.103 = bf16[256,4096]{1,0:T(8,128)(2,1)S(1)} fusion(bf16[1,768,4096]{2,1,0:T(8,128)(2,1)} %get-tuple-element.389, bf16[256,4096]{1,0:T(8,128)(2,1)} %copy-done.3, bf16[1,4096,768]{2,1,0:T(8,128)(2,1)} %get-tuple-element.388, f32[256,768]{1,0:T(8,128)S(1)} %fusion.102), kind=kOutput, calls=%fused_computation.13.clone.1 | convolution fusion | flops 3223453696 | bytes 17563648 | tf_op jit(solution)/shard_map/while/body/dot_general | solution.py:103
  525.3 13.3 %scatter_fusion = bf16[1281,4096]{1,0:T(8,128)(2,1)} fusion(bf16[1281,4096]{1,0:T(8,128)(2,1)} %get-tuple-element.371, s32[256]{0:T(256)S(1)} %compare_select_fusion.6, bf16[256,4096]{1,0:T(8,128)(2,1)S(1)} %fusion.103), kind=kCustom, calls=%fused_computation.3.clone.1 | custom fusion | bytes 6292480 | tf_op jit(solution)/shard_map/while/body/scatter | solution.py:124
  538.7 9.2 gather_fusion
  553.3 9.8 %fusion.103 = bf16[256,4096]{1,0:T(8,128)(2,1)S(1)} fusion(bf16[1,768,4096]{2,1,0:T(8,128)(2,1)} %get-tuple-element.389, bf16[256,4096]{1,0:T(8,128)(2,1)} %copy-done.3, bf16[1,4096,768]{2,1,0:T(8,128)(2,1)} %get-tuple-element.388, f32[256,768]{1,0:T(8,128)S(1)} %fusion.102), kind=kOutput, calls=%fused_computation.13.clone.1 | convolution fusion | flops 3223453696 | bytes 17563648 | tf_op jit(solution)/shard_map/while/body/dot_general | solution.py:103
  563.1 13.3 %scatter_fusion = bf16[1281,4096]{1,0:T(8,128)(2,1)} fusion(bf16[1281,4096]{1,0:T(8,128)(2,1)} %get-tuple-element.371, s32[256]{0:T(256)S(1)} %compare_select_fusion.6, bf16[256,4096]{1,0:T(8,128)(2,1)S(1)} %fusion.103), kind=kCustom, calls=%fused_computation.3.clone.1 | custom fusion | bytes 6292480 | tf_op jit(solution)/shard_map/while/body/scatter | solution.py:124
  576.4 9.6 %slice.69 = bf16[1280,4096]{1,0:T(8,128)(2,1)} slice(bf16[1281,4096]{1,0:T(8,128)(2,1)} %get-tuple-element.95), slice={[0:1280], [0:4096]} | slice | bytes 20971520 | tf_op jit(solution)/shard_map/slice | solution.py:127
  586.0 15.2 %reshape.244 = bf16[128,10,4096]{2,1,0:T(8,128)(2,1)} reshape(bf16[1280,4096]{1,0:T(8,128)(2,1)} %slice.69) | data formatting | bytes 20971520 | tf_op jit(solution)/shard_map/reshape | solution.py:127
  601.2 10.1 %all-to-all-start.6 = ((bf16[128,10,4096]{2,1,0:T(8,128)(2,1)}), bf16[128,10,4096]{2,1,0:T(8,128)(2,1)}, u32[]{:S(2)}, u32[]{:S(2)}) async-start(bf16[128,10,4096]{2,1,0:T(8,128)(2,1)} %reshape.244), calls=%async_computation.6 | async-start | bytes 33554432 | tf_op jit(solution)/shard_map/all_to_all | solution.py:158
  613.2 234.0 %all-to-all-done.6 = bf16[128,10,4096]{2,1,0:T(8,128)(2,1)} async-done(((bf16[128,10,4096]{2,1,0:T(8,128)(2,1)}), bf16[128,10,4096]{2,1,0:T(8,128)(2,1)}, u32[]{:S(2)}, u32[]{:S(2)}) %all-to-all-start.6) | async-done | bytes 10485792 | tf_op jit(solution)/shard_map/all_to_all | solution.py:158
  847.2 16.5 %reshape.245 = bf16[1280,4096]{1,0:T(8,128)(2,1)} reshape(bf16[128,10,4096]{2,1,0:T(8,128)(2,1)} %all-to-all-done.6) | data formatting | bytes 20971520 | tf_op jit(solution)/shard_map/reshape | solution.py:159
  863.8 20.4 %gather_fusion.2 = bf16[1024,4096]{1,0:T(8,128)(2,1)} fusion(bf16[1280,4096]{1,0:T(8,128)(2,1)} %reshape.245, s32[1024]{0:T(1024)S(1)} %broadcast_clamp_fusion), kind=kCustom, calls=%fused_computation.2 | custom fusion | bytes 16781312 | tf_op jit(solution)/shard_map/gather | solution.py:159
  884.2 39.5 %fusion.77 = (bf16[128,1,4096]{2,1,0:T(2,128)(2,1)S(1)}, bf16[128,1,4096]{2,1,0:T(2,128)(2,1)S(1)}, bf16[128,1,4096]{2,1,0:T(2,128)(2,1)S(1)}, bf16[128,1,4096]{...) fusion(bf16[128,8,4096]{2,1,0:T(8,128)(2,1)} %bitcast.183), kind=kLoop, calls=%fused_computation.151 | loop fusion | bytes 16777216 | tf_op jit(solution)/shard_map/slice | solution.py:162
  923.7 20.6 %fusion.45 = bf16[128,4096]{1,0:T(8,128)(2,1)} fusion(bf16[128,1,4096]{2,1,0:T(2,128)(2,1)} %get-tuple-element.203, bf16[128,1,4096]{2,1,0:T(2,128)(2,1)S(1)} %get-tuple-element.197, bf16[128,1,4096]{2,1,0:T(2,128)(2,1)S(1)} %get-tuple-element.198, bf16[128,1,4096]{2,1,0:T(2,128)(2,1)S(1)} %get-tuple-element.199, ...), kind=kLoop, calls=%fused_computation.59 | loop fusion | flops 12582912 | bytes 9441280 | tf_op jit(solution)/shard_map/convert_element_type | solution.py:163
  (178 shorter events, 105.2 us)
Async XLA Ops:
  7.2 0.8 copy-start
  7.2 28.6 %copy-start.6 = (s32[128,8]{0,1:T(8,128)S(1)}, s32[128,8]{0,1:T(8,128)}, u32[]{:S(2)}) copy-start(s32[128,8]{0,1:T(8,128)} %param.17) | copy-start | bytes 12292
  7.2 111.6 %all-gather.5.cloned.1.call-start = ((), (), s32[]{:S(2)}) async-start(), calls=%async_computation.8 | async-start | bytes 2359296 | tf_op jit(solution)/shard_map/all_gather | solution.py:67
  22.8 96.0 %all-gather.3.cloned.1.call-start = ((), (), s32[]{:S(2)}) async-start(), calls=%async_computation.7 | async-start | bytes 2359296 | tf_op jit(solution)/shard_map/all_gather | solution.py:66
  35.7 14.3 %copy-start.4 = (bf16[128,4096]{1,0:T(8,128)(2,1)S(1)}, bf16[128,4096]{1,0:T(8,128)(2,1)}, u32[]{:S(2)}) copy-start(bf16[128,4096]{1,0:T(8,128)(2,1)} %param.16) | copy-start | bytes 3145732
  37.2 0.6 copy-start.7
  42.9 32.2 %all-to-all-start.4 = ((s32[128,1,10]{2,1,0:T(1,128)}), s32[128,1,10]{2,1,0:T(1,128)S(1)}, u32[]{:S(2)}, u32[]{:S(2)}) async-start(s32[128,1,10]{2,1,0:T(1,128)} %bitcast.20), calls=%async_computation.4 | async-start | bytes 131072 | tf_op jit(solution)/shard_map/all_to_all | solution.py:153
  58.5 15.7 %copy-start.5 = (bf16[64,4096]{1,0:T(8,128)(2,1)S(1)}, bf16[64,4096]{1,0:T(8,128)(2,1)}, u32[]{:S(2)}) copy-start(bf16[64,4096]{1,0:T(8,128)(2,1)} %param.13) | copy-start | bytes 1572868
  75.0 17.9 %all-to-all-start.1 = ((bf16[64,16,256]{2,0,1:T(8,128)(2,1)}), bf16[64,16,256]{2,0,1:T(8,128)(2,1)S(1)}, u32[]{:S(2)}, u32[]{:S(2)}) async-start(bf16[64,16,256]{2,0,1:T(8,128)(2,1)} %bitcast.154), calls=%async_computation.1 | async-start | bytes 1048576 | tf_op jit(solution)/shard_map/all_to_all | solution.py:30
  92.9 256.4 %all-to-all-start.5 = ((bf16[128,10,4096]{2,1,0:T(8,128)(2,1)}), bf16[128,10,4096]{2,1,0:T(8,128)(2,1)}, u32[]{:S(2)}, u32[]{:S(2)}) async-start(bf16[128,10,4096]{2,1,0:T(8,128)(2,1)} %reshape.242), calls=%async_computation.5 | async-start | bytes 33554432 | tf_op jit(solution)/shard_map/all_to_all | solution.py:152
  125.5 5.9 copy-start.2
  140.4 5.9 copy-start.2
  155.2 5.9 copy-start.2
  170.1 5.9 copy-start.2
  185.0 5.9 copy-start.2
  199.8 5.9 copy-start.2
  214.7 5.9 copy-start.2
  229.5 5.9 copy-start.2
  349.3 251.9 %all-to-all-start.3 = ((bf16[16,64,256]{2,1,0:T(8,128)(2,1)}), bf16[16,64,256]{2,1,0:T(8,128)(2,1)}, u32[]{:S(2)}, u32[]{:S(2)}) async-start(bf16[16,64,256]{2,1,0:T(8,128)(2,1)} %all_to_all.79), calls=%async_computation.3 | async-start | bytes 1048576 | tf_op jit(solution)/shard_map/all_to_all | solution.py:96
  396.8 5.3 copy-start.3
  434.6 5.3 copy-start.3
  472.4 5.3 copy-start.3
  510.2 5.3 copy-start.3
  548.0 5.3 copy-start.3
  601.2 10.1 %copy-start.8 = (s32[1024,1]{0,1:T(1,128)S(1)}, s32[1024,1]{0,1:T(1,128)}, u32[]{:S(2)}) copy-start(s32[1024,1]{0,1:T(1,128)} %copy-done.7) | copy-start | bytes 12292
  601.2 10.1 %copy-start.9 = (f32[128,8]{0,1:T(8,128)S(1)}, f32[128,8]{0,1:T(8,128)}, u32[]{:S(2)}) copy-start(f32[128,8]{0,1:T(8,128)} %param.18) | copy-start | bytes 12292
  601.2 246.0 %all-to-all-start.6 = ((bf16[128,10,4096]{2,1,0:T(8,128)(2,1)}), bf16[128,10,4096]{2,1,0:T(8,128)(2,1)}, u32[]{:S(2)}, u32[]{:S(2)}) async-start(bf16[128,10,4096]{2,1,0:T(8,128)(2,1)} %reshape.244), calls=%async_computation.6 | async-start | bytes 33554432 | tf_op jit(solution)/shard_map/all_to_all | solution.py:158
  923.7 20.6 %copy-start.1 = (bf16[64,512]{1,0:T(8,128)(2,1)S(1)}, bf16[64,512]{1,0:T(8,128)(2,1)}, u32[]{:S(2)}) copy-start(bf16[64,512]{1,0:T(8,128)(2,1)} %param.15) | copy-start | bytes 196612
Sparse Core Ops, SparseCore 0:
  22.9 23.0 all-gather.4
  47.8 25.7 all-gather.2
where the time goes:
time: 960 us; the launch traced here: 951 us
  waiting for transfers between devices  346 us (36%)
  local copies, waits for them, and re-layouts  294 us (31%)
  matrix products  165 us (17%)
  starting transfers between devices  56.9 us (6%)
  other arithmetic  47.3 us (5%)
  blocking collectives  26.7 us (3%)
  between operations  15.3 us (2%)
    all_to_all x1, waiting for transfers between devices, mixture(): lax.all_to_all(served, ('ctx', 'exp'), split_axis=0, concat_axis=0, tiled...  234 us
    all_to_all x1, waiting for transfers between devices, mixture(): lax.all_to_all(payload[0], ('ctx', 'exp'), split_axis=0, concat_axis=0, t...  110 us
    scatter x5, local copies, waits for them, and re-layouts, one_block(): output.at[picked].set(expert_ffn(with_blank[picked], w_gate, w_up, w_down))  66.7 us
    dot_general x5, matrix products, expert_ffn(): jnp.dot(hidden, w_down[0], preferred_element_type=jnp.float32)  48.8 us
    dot_general x8, matrix products, block_step(): jnp.einsum('qhd,kd->hqk', query_grid, key_block, preferred_element_type=j...  47.5 us
    gather x5, local copies, waits for them, and re-layouts, one_block(): with_blank[picked]  46.2 us
    dot_general x8, matrix products, block_step(): jnp.einsum('hqk,kd->qhd', probs, value_block, preferred_element_type=jnp....  41.8 us
    slice x1, local copies, waits for them, and re-layouts, mixture(): gathered[:, slot, :].astype(jnp.float32)  39.5 us
  transfers between devices with their start and end apart: 7, of which 3 were waited for; matrix products, arithmetic and copies ran while one was open for 42% of the time, Pallas kernels for 0%

commit v1 on v0

v1 whole, which is shorter than its diff:
```python
import math

import jax
import jax.numpy as jnp
import numpy as np
from jax import lax
from jax.experimental import pallas as pl
from jax.experimental.pallas import tpu as pltpu
from jax.sharding import PartitionSpec as P

MESH = pl.DeviceIdType.MESH
BF = jnp.bfloat16
F32 = jnp.float32
D = 4096
FFE = 768
TOKENS = 128
SEQ = 64
PARTS = ((0, 0, 1536), (1, 1536, 1280), (2, 2816, 1280))
STEPS = (1, 3, 2)


def plane_offset(axis, i):
    d = [i // 4 % 4, i % 4]
    d.insert(axis, 0)
    return tuple(d) + (i // 16,)


def line_offset(axis, m):
    d = [0, 0, 0, 0]
    d[axis] = m
    return tuple(d)


def shuffled(core):
    order = [(p, i) for p in range(3) for i in range(16 * core, 16 * core + 16)]
    np.random.RandomState(3 + core).shuffle(order)
    return [(int(p), int(i)) for p, i in order if i > 0]


PEERS = sorted({plane_offset(p, i) for p in range(3) for i in range(1, 32)})


def place():
    c = lax.axis_index("ctx")
    e = lax.axis_index("exp")
    return c % 4, c // 4, e // 2, e % 2


def device(x, y, z, c):
    return (y * 4 + x, z * 2 + c)


def moved(d):
    x, y, z, c = place()
    return device((x + d[0]) % 4, (y + d[1]) % 4, (z + d[2]) % 4, (c + d[3]) % 2)


def moved_back(d):
    return moved(((-d[0]) % 4, (-d[1]) % 4, (-d[2]) % 4, d[3]))


def greet_all():
    barrier = pltpu.get_barrier_semaphore()
    for d in PEERS:
        pl.semaphore_signal(barrier, inc=1, device_id=moved(d), device_id_type=MESH)


def await_all():
    pl.semaphore_wait(pltpu.get_barrier_semaphore(), len(PEERS))


def remote(src, dst, send, recv, target):
    return pltpu.make_async_remote_copy(
        src_ref=src, dst_ref=dst, send_sem=send, recv_sem=recv, device_id=target, device_id_type=MESH
    )


def owners(axis):
    x, y, z, c = place()
    i = lax.broadcasted_iota(jnp.int32, (32, TOKENS), 0)
    d = [i // 4 % 4, i % 4]
    d.insert(axis, 0)
    chip = ((y + d[1]) % 4 * 4 + (x + d[0]) % 4) * 4 + (z + d[2]) % 4
    return (chip * 2 + (c + i // 16) % 2).astype(F32)


def ranks(ids, owner):
    named = jnp.zeros((32, TOKENS), F32)
    for k in range(8):
        named = named + jnp.where(ids[k : k + 1, :] == owner, 1.0, 0.0)
    shape = (TOKENS, TOKENS)
    before = lax.broadcasted_iota(jnp.int32, shape, 0) < lax.broadcasted_iota(jnp.int32, shape, 1)
    rank = jnp.dot(named.astype(BF), jnp.where(before, 1.0, 0.0).astype(BF), preferred_element_type=F32)
    return jnp.where(named > 0.5, rank, -1.0)


def spread(a):
    return jnp.broadcast_to(a[:, None, :], (32, 8, TOKENS)).reshape(256, TOKENS)


def line_index():
    return lax.broadcasted_iota(jnp.int32, (256, TOKENS), 0) % 8


def slot_masks(rank, m):
    row, line = spread(rank), line_index()
    early = row == line.astype(F32)
    late = (row == (8 + line % 2).astype(F32)) & (line // 2 == m)
    return early, late


def reorder(axis, forward):
    a = lax.broadcasted_iota(jnp.int32, (128, 128), 0 if forward else 1)
    b = lax.broadcasted_iota(jnp.int32, (128, 128), 1 if forward else 0)
    dx, dy, dz, s = a // 32, a // 8 % 4, a // 2 % 4, a % 2
    there = (dy * 4 + dz) * 8 + dx * 2 + s if axis == 0 else (dx * 4 + dz) * 8 + dy * 2 + s
    return jnp.where(there == b, 1.0, 0.0).astype(BF)


def kernel(
    q_ref, k_ref, v_ref, rows_ref, ids_ref, weight_ref, gate_ref, up_ref, down_ref,
    att_ref, mix_ref, recv_a, recv_b, recv_c, came_a, came_b, came_c,
    line_a, line_b, line_c, pack_a, pack_b, pack_c, ids_here, weights_here, info, meta, late_hot,
    kv, queries, v_turned, heads_out, work, gate, up, down, hidden, land, mixing, sum_a, sum_b, sum_c, own_sum,
    send_sem, recv_sem, line_send, line_recv, meta_send, meta_recv, in_send, in_recv,
    kv_send, kv_recv, core_send, core_recv, out_send, out_recv, local_sem,
    load_sem, w_sem, back_send, back_recv, sum_send, sum_recv, land_sem,
):
    x, y, z, c = place()
    ctx = y * 4 + x
    lines, packs, recvs = (line_a, line_b, line_c), (pack_a, pack_b, pack_c), (recv_a, recv_b, recv_c)
    cames, sums = (came_a, came_b, came_c), (sum_a, sum_b, sum_c)
    greet_all()
    small = [
        pltpu.make_async_copy(ids_ref, ids_here, land_sem.at[0]),
        pltpu.make_async_copy(weight_ref, weights_here, land_sem.at[1]),
    ]
    for copy in small:
        copy.start()
    mine = [
        pltpu.make_async_copy(rows_ref.at[:, at : at + width], lines[axis].at[pl.ds(0, TOKENS)], local_sem.at[7 + axis])
        for axis, at, width in PARTS
    ]
    for copy in mine:
        copy.start()
    for copy in small:
        copy.wait()
    info[0:8, :] = ids_here[...].astype(F32)
    info[8:16, :] = weights_here[...]
    await_all()

    along = {}
    for n, m in enumerate(STEPS):
        for axis, at, width in PARTS:
            target = moved(line_offset(axis, m))
            i = 3 * n + axis
            told = remote(info, meta.at[axis, m], meta_send.at[i], meta_recv.at[i], target)
            told.start()
            data = remote(
                rows_ref.at[:, at : at + width], lines[axis].at[pl.ds(TOKENS * m, TOKENS)],
                line_send.at[i], line_recv.at[i], target,
            )
            data.start()
            along[axis, m] = (told, data)

    first = []
    for dz in range(1, 4):
        zt = (z + dz) % 4
        target = device(x, y, zt, c)
        for n, (src, dst) in enumerate(
            (
                (k_ref.at[:, pl.ds(zt * 128, 128)], kv.at[ctx, z, c, :, pl.ds(0, 128)]),
                (v_ref.at[:, pl.ds(zt * 128, 128)], kv.at[ctx, z, c, :, pl.ds(128, 128)]),
                (q_ref.at[:, pl.ds(zt * 1024, 1024)], queries.at[z]),
            )
        ):
            i = (dz - 1) * 3 + n
            first.append(remote(src, dst, in_send.at[i], in_recv.at[i], target))
            first[-1].start()
    own = (
        (k_ref.at[:, pl.ds(z * 128, 128)], kv.at[ctx, z, c, :, pl.ds(0, 128)]),
        (v_ref.at[:, pl.ds(z * 128, 128)], kv.at[ctx, z, c, :, pl.ds(128, 128)]),
        (q_ref.at[:, pl.ds(z * 1024, 1024)], queries.at[z]),
    )
    for i, (src, dst) in enumerate(own):
        first.append(pltpu.make_async_copy(src, dst, local_sem.at[i]))
        first[-1].start()

    weights = [
        pltpu.make_async_copy(gate_ref.at[0], gate, w_sem.at[0]),
        pltpu.make_async_copy(up_ref.at[0], up, w_sem.at[1]),
        pltpu.make_async_copy(down_ref.at[0], down, w_sem.at[2]),
    ]
    for copy in weights:
        copy.start()

    for m in (0,) + STEPS:
        for axis, at, width in PARTS:
            if m == 0:
                meta[axis, 0] = info[...]
                mine[axis].wait()
            else:
                for copy in along[axis, m]:
                    copy.wait()
            early, late = slot_masks(ranks(meta[axis, m], owners(axis)), m)
            hot = jnp.where(early, 1.0, 0.0).astype(BF)
            late_hot[axis, :, TOKENS * m : TOKENS * (m + 1)] = jnp.where(late, 1.0, 0.0).astype(BF)
            packs[axis][m] = jnp.dot(
                hot, lines[axis][TOKENS * m : TOKENS * (m + 1), :], preferred_element_type=F32
            ).astype(BF)
    for copy in first:
        copy.wait()
    for k in range(1, 16):

        @pl.when(ctx + k < 16)
        def _():
            there = ctx + k
            remote(
                kv.at[ctx, :, c], kv.at[ctx, :, c], kv_send.at[k - 1], kv_recv.at[k - 1], (there, z * 2 + c)
            ).start()

    for axis, at, width in PARTS:
        packs[axis][4] = jnp.dot(late_hot[axis], lines[axis][...], preferred_element_type=F32).astype(BF)

    sends = ([], [])
    stays = []
    for core in range(2):
        for axis, i in shuffled(core):
            cut = pl.ds(8 * i, 8)
            n = 31 * axis + i - 1
            sends[core].append(
                remote(
                    packs[axis].at[:, cut], recvs[axis].at[:, cut],
                    send_sem.at[n], recv_sem.at[n], moved(plane_offset(axis, i)),
                )
            )
            sends[core][-1].start()
    for axis in range(3):
        cut = pl.ds(0, 8)
        stays.append(pltpu.make_async_copy(packs[axis].at[:, cut], recvs[axis].at[:, cut], local_sem.at[3 + axis]))
        stays[-1].start()

    for k in range(1, 16):
        copy = remote(
            kv.at[ctx, :, c], kv.at[ctx, :, c], kv_send.at[k - 1], kv_recv.at[k - 1], (ctx, z * 2 + c)
        )

        @pl.when(ctx >= k)
        def _():
            copy.wait_recv()

        @pl.when(ctx + k < 16)
        def _():
            copy.wait_send()

    def core_copy(j):
        return remote(
            kv.at[j, :, c], kv.at[j, :, c], core_send.at[j], core_recv.at[j], device(x, y, z, 1 - c)
        )

    def core_start(j, carry):
        core_copy(j).start()
        return carry

    def core_wait(j, carry):
        core_copy(j).wait()
        return carry

    lax.fori_loop(0, ctx + 1, core_start, 0)
    lax.fori_loop(0, ctx + 1, core_wait, 0)

    def turn(j, carry):
        block = kv[j].reshape(512, 256)
        v_turned[j] = block[:, 128:256].astype(F32).T.astype(BF)
        return carry

    lax.fori_loop(0, ctx + 1, turn, 0)
    factor = math.log2(math.e) / math.sqrt(128.0)
    column = lax.broadcasted_iota(jnp.int32, (512, 256), 1)
    allowed = lax.broadcasted_iota(jnp.int32, (512, 256), 0) <= (column // 64 * 2 + c) * 64 + column % 64

    def head(h, carry):
        cut = pl.ds(pl.multiple_of(h * 128, 128), 128)
        q = queries[:, :, cut].reshape(256, 128)

        def step(j, state, masked):
            row_max, row_sum, total = state
            key = kv[j].reshape(512, 256)[:, 0:128]
            score = lax.dot_general(key, q, (((1,), (1,)), ((), ())), preferred_element_type=F32) * factor
            if masked:
                score = jnp.where(allowed, score, -1e30)
            new_max = jnp.maximum(row_max, jnp.max(score, axis=0, keepdims=True))
            prob = jnp.exp2(score - new_max)
            old = jnp.exp2(row_max - new_max)
            row_sum = row_sum * old + jnp.sum(prob, axis=0, keepdims=True)
            total = total * old + jnp.dot(v_turned[j], prob.astype(BF), preferred_element_type=F32)
            return (new_max, row_sum, total)

        state = (
            jnp.full((1, 256), -1e30, F32),
            jnp.zeros((1, 256), F32),
            jnp.zeros((128, 256), F32),
        )
        state = step(ctx, state, True)
        state = lax.fori_loop(0, ctx, lambda j, s: step(j, s, False), state)
        result = (state[2] / state[1]).T
        heads_out[:, :, cut] = result.reshape(4, 64, 128).astype(BF)
        return carry

    lax.fori_loop(0, 8, head, 0)
    last = []
    for dz in range(1, 4):
        zt = (z + dz) % 4
        last.append(
            remote(
                heads_out.at[zt], att_ref.at[:, pl.ds(z * 1024, 1024)],
                out_send.at[dz - 1], out_recv.at[dz - 1], device(x, y, zt, c),
            )
        )
        last[-1].start()
    last.append(pltpu.make_async_copy(heads_out.at[z], att_ref.at[:, pl.ds(z * 1024, 1024)], local_sem.at[6]))
    last[-1].start()

    def load(core):
        at = 128 * core
        for dx in range(4):
            pltpu.make_async_copy(
                recv_a.at[dx, pl.ds(at, 128)], work.at[pl.ds(128 * dx, 128), 0:1536], load_sem.at[0]
            ).start()
        pltpu.make_async_copy(recv_a.at[4, pl.ds(at, 128)], work.at[pl.ds(512, 128), 0:1536], load_sem.at[0]).start()
        for n in range(16):
            pltpu.make_async_copy(
                recv_b.at[n % 4, pl.ds(at + n // 4 * 32, 32)], work.at[pl.ds(32 * n, 32), 1536:2816], load_sem.at[0]
            ).start()
        pltpu.make_async_copy(recv_b.at[4, pl.ds(at, 128)], work.at[pl.ds(512, 128), 1536:2816], load_sem.at[0]).start()

        def piece(n, carry):
            pltpu.make_async_copy(
                recv_c.at[n % 4, pl.ds(pl.multiple_of(at + n // 4 * 8, 8), 8)],
                work.at[pl.ds(pl.multiple_of(8 * n, 8), 8), 2816:4096],
                load_sem.at[0],
            ).start()
            return carry

        lax.fori_loop(0, 64, piece, 0)
        pltpu.make_async_copy(recv_c.at[4, pl.ds(at, 128)], work.at[pl.ds(512, 128), 2816:4096], load_sem.at[0]).start()

    returns = []
    for core in range(2):
        for copy in sends[core]:
            copy.wait_recv()
        if core == 0:
            for copy in stays:
                copy.wait()
        load(core)
        pltpu.make_async_copy(work, work, load_sem.at[0]).wait()
        if core == 0:
            weights[0].wait()
            weights[1].wait()
        for axis, at, width in PARTS[:2]:
            work[512:640, at : at + width] = jnp.dot(
                reorder(axis, True), work[512:640, at : at + width], preferred_element_type=F32
            ).astype(BF)

        def inner(n, carry):
            cut = pl.ds(pl.multiple_of(n * 256, 256), 256)
            a = jnp.dot(work[...], gate[:, cut], preferred_element_type=F32)
            b = jnp.dot(work[...], up[:, cut], preferred_element_type=F32)
            hidden[:, cut] = (a / (1.0 + jnp.exp(-a)) * b).astype(BF)
            return carry

        lax.fori_loop(0, 3, inner, 0)
        if core == 0:
            weights[2].wait()
        for copy in sends[core]:
            copy.wait_send()
        for axis, at, width in PARTS:
            ref = packs[axis]

            def outer(n, carry):
                cut = pl.ds(pl.multiple_of(n * 256, 256), 256)
                from_cut = pl.ds(pl.multiple_of(at + n * 256, 256), 256)
                value = jnp.dot(hidden[...], down[:, from_cut], preferred_element_type=F32)
                row = 128 * core
                if axis == 0:
                    for dx in range(4):
                        ref[dx, row : row + 128, cut] = value[128 * dx : 128 * (dx + 1)].astype(BF)
                elif axis == 1:
                    for n2 in range(16):
                        to = row + n2 // 4 * 32
                        ref[n2 % 4, to : to + 32, cut] = value[32 * n2 : 32 * (n2 + 1)].astype(BF)
                else:
                    for n2 in range(64):
                        to = row + n2 // 4 * 8
                        ref[n2 % 4, to : to + 8, cut] = value[8 * n2 : 8 * (n2 + 1)].astype(BF)
                late = value[512:640].astype(BF)
                if axis < 2:
                    late = jnp.dot(reorder(axis, False), late, preferred_element_type=F32).astype(BF)
                ref[4, row : row + 128, cut] = late
                return carry

            lax.fori_loop(0, width // 256, outer, 0)
        for axis, i in shuffled(core):
            cut = pl.ds(8 * i, 8)
            n = 31 * axis + i - 1
            returns.append(
                remote(
                    packs[axis].at[:, cut], cames[axis].at[:, cut],
                    back_send.at[n], back_recv.at[n], moved_back(plane_offset(axis, i)),
                )
            )
            returns[-1].start()
        if core == 0:
            for axis in range(3):
                cut = pl.ds(0, 8)
                returns.append(
                    pltpu.make_async_copy(packs[axis].at[:, cut], cames[axis].at[:, cut], local_sem.at[3 + axis])
                )
                returns[-1].start()

    for axis, at, width in PARTS:
        for m in range(4):
            early, late = slot_masks(ranks(meta[axis, m], owners(axis)), m)
            value = jnp.zeros((32, TOKENS), F32)
            for k in range(8):
                value = value + jnp.where(
                    meta[axis, m, k : k + 1, :] == owners(axis), meta[axis, m, 8 + k : 9 + k, :], 0.0
                )
            value = spread(value)
            for n, mask in enumerate((early, late)):
                turned = jnp.where(mask, value, 0.0).T
                high = turned.astype(BF)
                mixing[axis, m, 0:TOKENS, 256 * n : 256 * (n + 1)] = high
                mixing[axis, m, TOKENS : 2 * TOKENS, 256 * n : 256 * (n + 1)] = (turned - high.astype(F32)).astype(BF)
    for copy in returns:
        copy.wait()

    tiles = [(axis, n) for axis, at, width in PARTS for n in range(width // 256)]

    def fetch(t):
        axis, n = tiles[t]
        return pltpu.make_async_copy(
            cames[axis].at[:, :, 256 * n : 256 * (n + 1)], land.at[t % 2], land_sem.at[t % 2]
        )

    parts = []
    fetch(0).start()
    for t, (axis, n) in enumerate(tiles):
        if t + 1 < len(tiles):
            fetch(t + 1).start()
        fetch(t).wait()
        cut = slice(256 * n, 256 * (n + 1))
        for m in STEPS + (0,):
            both = jnp.dot(mixing[axis, m, :, 0:256], land[t % 2, m], preferred_element_type=F32)
            both = both + jnp.dot(mixing[axis, m, :, 256:512], land[t % 2, 4], preferred_element_type=F32)
            total = both[0:TOKENS] + both[TOKENS : 2 * TOKENS]
            if m == 0:
                at = PARTS[axis][1] + 256 * n
                own_sum[:, at : at + 256] = total
            else:
                lines[axis][TOKENS * m : TOKENS * (m + 1), cut] = total.astype(BF)
        if n == PARTS[axis][2] // 256 - 1:
            for s, m in enumerate(STEPS):
                i = 3 * s + axis
                parts.append(
                    remote(
                        lines[axis].at[pl.ds(TOKENS * m, TOKENS)], sums[axis].at[s], sum_send.at[i], sum_recv.at[i],
                        moved_back(line_offset(axis, m)),
                    )
                )
                parts[-1].start()
    for copy in last:
        copy.wait()
    for copy in parts:
        copy.wait()
    for axis, at, width in PARTS:
        total = own_sum[:, at : at + width]
        for s in range(3):
            total = total + sums[axis][s].astype(F32)
        work[0:TOKENS, at : at + width] = total.astype(BF)
    result = pltpu.make_async_copy(work.at[pl.ds(0, TOKENS)], mix_ref, local_sem.at[0])
    result.start()
    result.wait()


def body(
    queries, rotated_key_heads, stacked_value_heads, moe_rows, expert_ids, route_weights, w_gate, w_up, w_down
):
    hbm = pl.BlockSpec(memory_space=pl.ANY)
    dma = pltpu.SemaphoreType.DMA
    widths = [width for _, _, width in PARTS]
    results = pl.pallas_call(
        kernel,
        out_shape=(jax.ShapeDtypeStruct((SEQ, D), BF), jax.ShapeDtypeStruct((TOKENS, D), BF))
        + tuple(jax.ShapeDtypeStruct((5, 256, w), BF) for w in widths) * 2,
        in_specs=[hbm] * 9,
        out_specs=(hbm,) * 8,
        scratch_shapes=[pltpu.VMEM((4 * TOKENS, w), BF) for w in widths]
        + [pltpu.VMEM((5, 256, w), BF) for w in widths]
        + [
            pltpu.VMEM((8, TOKENS), jnp.int32),
            pltpu.VMEM((8, TOKENS), F32),
            pltpu.VMEM((16, TOKENS), F32),
            pltpu.VMEM((3, 4, 16, TOKENS), F32),
            pltpu.VMEM((3, 256, 4 * TOKENS), BF),
            pltpu.VMEM((16, 4, 2, SEQ, 256), BF),
            pltpu.VMEM((4, SEQ, 1024), BF),
            pltpu.VMEM((16, 128, 512), BF),
            pltpu.VMEM((4, SEQ, 1024), BF),
            pltpu.VMEM((640, D), BF),
            pltpu.VMEM((D, FFE), BF),
            pltpu.VMEM((D, FFE), BF),
            pltpu.VMEM((FFE, D), BF),
            pltpu.VMEM((640, FFE), BF),
            pltpu.VMEM((2, 5, 256, 256), BF),
            pltpu.VMEM((3, 4, 2 * TOKENS, 512), BF),
        ]
        + [pltpu.VMEM((3, TOKENS, w), BF) for w in widths]
        + [pltpu.VMEM((TOKENS, D), F32)]
        + [dma((n,)) for n in (93, 93, 9, 9, 9, 9, 9, 9, 15, 15, 16, 16, 3, 3, 10)]
        + [dma((n,)) for n in (1, 3, 93, 93, 9, 9, 2)],
        compiler_params=pltpu.CompilerParams(
            collective_id=0, has_side_effects=True, vmem_limit_bytes=62 * 2**20
        ),
        name="attend_and_mix",
    )(
        queries, rotated_key_heads, stacked_value_heads, moe_rows, expert_ids.T, route_weights.T,
        w_gate, w_up, w_down,
    )
    return results[0], results[1]


def solution(mesh):
    rows = P(("ctx", "exp"), None)
    cube = P(("ctx", "exp"), None, None)
    return jax.shard_map(
        body,
        mesh=mesh,
        in_specs=(rows,) * 6 + (cube,) * 3,
        out_specs=(rows, rows),
        check_vma=False,
    )
```

time: 960 us -> 286 us (0.30)
  the two profiles are of different devices: /device:TPU:66 before, /device:TPU:1 now
where the time goes in v1:
time: 286 us; the launch traced here: 281 us
  Pallas kernels  276 us (97%)
  local copies, waits for them, and re-layouts  4.16 us (1%)
    pallas_call x1, Pallas kernels, body(): pl.pallas_call(kernel, out_shape=(jax.ShapeDtypeStruct((SEQ, D), BF), jax...  276 us

profile of v1, /device:TPU:1, one launch (start us, length us, event | category | flops | bytes accessed | tf_op | source)
XLA Modules:
  0.0 281.3 jit_solution(4936858803825031050)
XLA Ops:
  0.6 276.5 %attend_and_mix.1 = (bf16[64,4096]{1,0:T(8,128)(2,1)}, bf16[128,4096]{1,0:T(8,128)(2,1)}, bf16[5,256,1536]{2,1,0:T(8,128)(2,1)}, bf16[5,256,1280]{2,1,0:T(8,128)...) custom-call(bf16[64,4096]{1,0:T(8,128)(2,1)} %q_ref.1, ...), custom_call_target="tpu_custom_call" | custom-call | tf_op jit(solution)/shard_map/attend_and_mix/pallas_call | solution.py:492
  277.1 1.9 copy.13
  279.0 2.3 copy.14

commit v2 on v1

--- a/solution.py
+++ b/solution.py
@@ -149,6 +149,19 @@
     info[8:16, :] = weights_here[...]
     await_all()
 
+    first = []
+    for dz in range(4):
+        zt = (z + dz) % 4
+        for n, ref in enumerate((k_ref, v_ref)):
+            there = ref.at[:, pl.ds(zt * 128, 128)]
+            here = kv.at[ctx, z, c, :, pl.ds(128 * n, 128)]
+            if dz == 0:
+                first.append(pltpu.make_async_copy(there, here, local_sem.at[n]))
+            else:
+                i = (dz - 1) * 3 + n
+                first.append(remote(there, here, in_send.at[i], in_recv.at[i], device(x, y, zt, c)))
+            first[-1].start()
+
     along = {}
     for n, m in enumerate(STEPS):
         for axis, at, width in PARTS:
@@ -163,28 +176,16 @@
             data.start()
             along[axis, m] = (told, data)
 
-    first = []
-    for dz in range(1, 4):
-        zt = (z + dz) % 4
-        target = device(x, y, zt, c)
-        for n, (src, dst) in enumerate(
-            (
-                (k_ref.at[:, pl.ds(zt * 128, 128)], kv.at[ctx, z, c, :, pl.ds(0, 128)]),
-                (v_ref.at[:, pl.ds(zt * 128, 128)], kv.at[ctx, z, c, :, pl.ds(128, 128)]),
-                (q_ref.at[:, pl.ds(zt * 1024, 1024)], queries.at[z]),
-            )
-        ):
-            i = (dz - 1) * 3 + n
-            first.append(remote(src, dst, in_send.at[i], in_recv.at[i], target))
-            first[-1].start()
-    own = (
-        (k_ref.at[:, pl.ds(z * 128, 128)], kv.at[ctx, z, c, :, pl.ds(0, 128)]),
-        (v_ref.at[:, pl.ds(z * 128, 128)], kv.at[ctx, z, c, :, pl.ds(128, 128)]),
-        (q_ref.at[:, pl.ds(z * 1024, 1024)], queries.at[z]),
-    )
-    for i, (src, dst) in enumerate(own):
-        first.append(pltpu.make_async_copy(src, dst, local_sem.at[i]))
-        first[-1].start()
+    for copy in first:
+        copy.wait()
+    for k in range(1, 16):
+
+        @pl.when(ctx + k < 16)
+        def _():
+            there = ctx + k
+            remote(
+                kv.at[ctx, :, c], kv.at[ctx, :, c], kv_send.at[k - 1], kv_recv.at[k - 1], (there, z * 2 + c)
+            ).start()
 
     weights = [
         pltpu.make_async_copy(gate_ref.at[0], gate, w_sem.at[0]),
@@ -208,17 +209,6 @@
             packs[axis][m] = jnp.dot(
                 hot, lines[axis][TOKENS * m : TOKENS * (m + 1), :], preferred_element_type=F32
             ).astype(BF)
-    for copy in first:
-        copy.wait()
-    for k in range(1, 16):
-
-        @pl.when(ctx + k < 16)
-        def _():
-            there = ctx + k
-            remote(
-                kv.at[ctx, :, c], kv.at[ctx, :, c], kv_send.at[k - 1], kv_recv.at[k - 1], (there, z * 2 + c)
-            ).start()
-
     for axis, at, width in PARTS:
         packs[axis][4] = jnp.dot(late_hot[axis], lines[axis][...], preferred_element_type=F32).astype(BF)
 
@@ -240,86 +230,16 @@
         stays.append(pltpu.make_async_copy(packs[axis].at[:, cut], recvs[axis].at[:, cut], local_sem.at[3 + axis]))
         stays[-1].start()
 
-    for k in range(1, 16):
-        copy = remote(
-            kv.at[ctx, :, c], kv.at[ctx, :, c], kv_send.at[k - 1], kv_recv.at[k - 1], (ctx, z * 2 + c)
-        )
-
-        @pl.when(ctx >= k)
-        def _():
-            copy.wait_recv()
-
-        @pl.when(ctx + k < 16)
-        def _():
-            copy.wait_send()
-
-    def core_copy(j):
-        return remote(
-            kv.at[j, :, c], kv.at[j, :, c], core_send.at[j], core_recv.at[j], device(x, y, z, 1 - c)
-        )
-
-    def core_start(j, carry):
-        core_copy(j).start()
-        return carry
-
-    def core_wait(j, carry):
-        core_copy(j).wait()
-        return carry
-
-    lax.fori_loop(0, ctx + 1, core_start, 0)
-    lax.fori_loop(0, ctx + 1, core_wait, 0)
-
-    def turn(j, carry):
-        block = kv[j].reshape(512, 256)
-        v_turned[j] = block[:, 128:256].astype(F32).T.astype(BF)
-        return carry
-
-    lax.fori_loop(0, ctx + 1, turn, 0)
-    factor = math.log2(math.e) / math.sqrt(128.0)
-    column = lax.broadcasted_iota(jnp.int32, (512, 256), 1)
-    allowed = lax.broadcasted_iota(jnp.int32, (512, 256), 0) <= (column // 64 * 2 + c) * 64 + column % 64
-
-    def head(h, carry):
-        cut = pl.ds(pl.multiple_of(h * 128, 128), 128)
-        q = queries[:, :, cut].reshape(256, 128)
-
-        def step(j, state, masked):
-            row_max, row_sum, total = state
-            key = kv[j].reshape(512, 256)[:, 0:128]
-            score = lax.dot_general(key, q, (((1,), (1,)), ((), ())), preferred_element_type=F32) * factor
-            if masked:
-                score = jnp.where(allowed, score, -1e30)
-            new_max = jnp.maximum(row_max, jnp.max(score, axis=0, keepdims=True))
-            prob = jnp.exp2(score - new_max)
-            old = jnp.exp2(row_max - new_max)
-            row_sum = row_sum * old + jnp.sum(prob, axis=0, keepdims=True)
-            total = total * old + jnp.dot(v_turned[j], prob.astype(BF), preferred_element_type=F32)
-            return (new_max, row_sum, total)
-
-        state = (
-            jnp.full((1, 256), -1e30, F32),
-            jnp.zeros((1, 256), F32),
-            jnp.zeros((128, 256), F32),
-        )
-        state = step(ctx, state, True)
-        state = lax.fori_loop(0, ctx, lambda j, s: step(j, s, False), state)
-        result = (state[2] / state[1]).T
-        heads_out[:, :, cut] = result.reshape(4, 64, 128).astype(BF)
-        return carry
-
-    lax.fori_loop(0, 8, head, 0)
-    last = []
-    for dz in range(1, 4):
+    asked = []
+    for dz in range(4):
         zt = (z + dz) % 4
-        last.append(
-            remote(
-                heads_out.at[zt], att_ref.at[:, pl.ds(z * 1024, 1024)],
-                out_send.at[dz - 1], out_recv.at[dz - 1], device(x, y, zt, c),
-            )
-        )
-        last[-1].start()
-    last.append(pltpu.make_async_copy(heads_out.at[z], att_ref.at[:, pl.ds(z * 1024, 1024)], local_sem.at[6]))
-    last[-1].start()
+        there = q_ref.at[:, pl.ds(zt * 1024, 1024)]
+        if dz == 0:
+            asked.append(pltpu.make_async_copy(there, queries.at[z], local_sem.at[2]))
+        else:
+            i = (dz - 1) * 3 + 2
+            asked.append(remote(there, queries.at[z], in_send.at[i], in_recv.at[i], device(x, y, zt, c)))
+        asked[-1].start()
 
     def load(core):
         at = 128 * core
@@ -432,10 +352,95 @@
                 high = turned.astype(BF)
                 mixing[axis, m, 0:TOKENS, 256 * n : 256 * (n + 1)] = high
                 mixing[axis, m, TOKENS : 2 * TOKENS, 256 * n : 256 * (n + 1)] = (turned - high.astype(F32)).astype(BF)
+    for copy in asked:
+        copy.wait()
+    for k in range(1, 16):
+        copy = remote(
+            kv.at[ctx, :, c], kv.at[ctx, :, c], kv_send.at[k - 1], kv_recv.at[k - 1], (ctx, z * 2 + c)
+        )
+
+        @pl.when(ctx >= k)
+        def _():
+            copy.wait_recv()
+
+        @pl.when(ctx + k < 16)
+        def _():
+            copy.wait_send()
+
+    def core_copy(j):
+        return remote(
+            kv.at[j, :, c], kv.at[j, :, c], core_send.at[j], core_recv.at[j], device(x, y, z, 1 - c)
+        )
+
+    def core_start(j, carry):
+        core_copy(j).start()
+        return carry
+
+    def core_wait(j, carry):
+        core_copy(j).wait()
+        return carry
+
+    lax.fori_loop(0, ctx + 1, core_start, 0)
+    lax.fori_loop(0, ctx + 1, core_wait, 0)
+
+    def turn(j, carry):
+        block = kv[j].reshape(512, 256)
+        v_turned[j] = block[:, 128:256].astype(F32).T.astype(BF)
+        return carry
+
+    lax.fori_loop(0, ctx + 1, turn, 0)
+    factor = math.log2(math.e) / math.sqrt(128.0)
+    column = lax.broadcasted_iota(jnp.int32, (512, 256), 1)
+    allowed = lax.broadcasted_iota(jnp.int32, (512, 256), 0) <= (column // 64 * 2 + c) * 64 + column % 64
+
+    def head(h, carry):
+        cut = pl.ds(pl.multiple_of(h * 128, 128), 128)
+        q = queries[:, :, cut].reshape(256, 128)
+
+        def step(j, state, masked):
+            row_max, row_sum, total = state
+            key = kv[j].reshape(512, 256)[:, 0:128]
+            score = lax.dot_general(key, q, (((1,), (1,)), ((), ())), preferred_element_type=F32) * factor
+            if masked:
+                score = jnp.where(allowed, score, -1e30)
+            new_max = jnp.maximum(row_max, jnp.max(score, axis=0, keepdims=True))
+            prob = jnp.exp2(score - new_max)
+            old = jnp.exp2(row_max - new_max)
+            row_sum = row_sum * old + jnp.sum(prob, axis=0, keepdims=True)
+            total = total * old + jnp.dot(v_turned[j], prob.astype(BF), preferred_element_type=F32)
+            return (new_max, row_sum, total)
+
+        state = (
+            jnp.full((1, 256), -1e30, F32),
+            jnp.zeros((1, 256), F32),
+            jnp.zeros((128, 256), F32),
+        )
+        state = step(ctx, state, True)
+        state = lax.fori_loop(0, ctx, lambda j, s: step(j, s, False), state)
+        result = (state[2] / state[1]).T
+        heads_out[:, :, cut] = result.reshape(4, 64, 128).astype(BF)
+        return carry
+
+    lax.fori_loop(0, 8, head, 0)
+    last = []
+    for dz in range(1, 4):
+        zt = (z + dz) % 4
+        last.append(
+            remote(
+                heads_out.at[zt], att_ref.at[:, pl.ds(z * 1024, 1024)],
+                out_send.at[dz - 1], out_recv.at[dz - 1], device(x, y, zt, c),
+            )
+        )
+        last[-1].start()
+    last.append(pltpu.make_async_copy(heads_out.at[z], att_ref.at[:, pl.ds(z * 1024, 1024)], local_sem.at[6]))
+    last[-1].start()
     for copy in returns:
         copy.wait()
 
-    tiles = [(axis, n) for axis, at, width in PARTS for n in range(width // 256)]
+    groups = [(axis, n) for n in (0, 3) for axis in range(3)]
+    tiles = [
+        (axis, n) for axis, first_tile in groups for n in range(first_tile, min(first_tile + 3, PARTS[axis][2] // 256))
+    ]
 
     def fetch(t):
         axis, n = tiles[t]
@@ -459,13 +464,14 @@
                 own_sum[:, at : at + 256] = total
             else:
                 lines[axis][TOKENS * m : TOKENS * (m + 1), cut] = total.astype(BF)
-        if n == PARTS[axis][2] // 256 - 1:
+        if n in (2, PARTS[axis][2] // 256 - 1):
+            half = slice(0, 768) if n == 2 else slice(768, PARTS[axis][2])
             for s, m in enumerate(STEPS):
-                i = 3 * s + axis
+                i = 3 * s + axis + (9 if n > 2 else 0)
                 parts.append(
                     remote(
-                        lines[axis].at[pl.ds(TOKENS * m, TOKENS)], sums[axis].at[s], sum_send.at[i], sum_recv.at[i],
-                        moved_back(line_offset(axis, m)),
+                        lines[axis].at[pl.ds(TOKENS * m, TOKENS), half], sums[axis].at[s, :, half],
+                        sum_send.at[i], sum_recv.at[i], moved_back(line_offset(axis, m)),
                     )
                 )
                 parts[-1].start()
@@ -518,7 +524,7 @@
         + [pltpu.VMEM((3, TOKENS, w), BF) for w in widths]
         + [pltpu.VMEM((TOKENS, D), F32)]
         + [dma((n,)) for n in (93, 93, 9, 9, 9, 9, 9, 9, 15, 15, 16, 16, 3, 3, 10)]
-        + [dma((n,)) for n in (1, 3, 93, 93, 9, 9, 2)],
+        + [dma((n,)) for n in (1, 3, 93, 93, 18, 18, 2)],
         compiler_params=pltpu.CompilerParams(
             collective_id=0, has_side_effects=True, vmem_limit_bytes=62 * 2**20
         ),

time: 286 us -> 277 us (0.969)
  the two profiles are of different devices: /device:TPU:1 before, /device:TPU:30 now
where the time goes in v2:
time: 277 us
  Pallas kernels  272 us (98%)
  local copies, waits for them, and re-layouts  4.16 us (2%)
    pallas_call x1, Pallas kernels, body(): pl.pallas_call(kernel, out_shape=(jax.ShapeDtypeStruct((SEQ, D), BF), jax...  272 us

profile of v2, /device:TPU:30, one launch (start us, length us, event | category | flops | bytes accessed | tf_op | source)
XLA Modules:
  0.0 276.7 jit_solution(5767496105074107798)
XLA Ops:
  0.6 271.9 %attend_and_mix.1 = (bf16[64,4096]{1,0:T(8,128)(2,1)}, bf16[128,4096]{1,0:T(8,128)(2,1)}, bf16[5,256,1536]{2,1,0:T(8,128)(2,1)}, bf16[5,256,1280]{2,1,0:T(8,128)...) custom-call(bf16[64,4096]{1,0:T(8,128)(2,1)} %q_ref.1, ...), custom_call_target="tpu_custom_call" | custom-call | tf_op jit(solution)/shard_map/attend_and_mix/pallas_call | solution.py:498
  272.5 1.9 copy.13
  274.4 2.3 copy.14

commit v3 on v1

--- a/solution.py
+++ b/solution.py
@@ -20,8 +20,9 @@
 
 
 def plane_offset(axis, i):
-    d = [i // 4 % 4, i % 4]
-    d.insert(axis, 0)
+    d = [0, 0, 0]
+    d[(axis + 1) % 3] = i // 4 % 4
+    d[(axis + 2) % 3] = i % 4
     return tuple(d) + (i // 16,)
 
 
@@ -78,8 +79,9 @@
 def owners(axis):
     x, y, z, c = place()
     i = lax.broadcasted_iota(jnp.int32, (32, TOKENS), 0)
-    d = [i // 4 % 4, i % 4]
-    d.insert(axis, 0)
+    d = [0, 0, 0]
+    d[(axis + 1) % 3] = i // 4 % 4
+    d[(axis + 2) % 3] = i % 4
     chip = ((y + d[1]) % 4 * 4 + (x + d[0]) % 4) * 4 + (z + d[2]) % 4
     return (chip * 2 + (c + i // 16) % 2).astype(F32)
 
@@ -113,23 +115,24 @@
     a = lax.broadcasted_iota(jnp.int32, (128, 128), 0 if forward else 1)
     b = lax.broadcasted_iota(jnp.int32, (128, 128), 1 if forward else 0)
     dx, dy, dz, s = a // 32, a // 8 % 4, a // 2 % 4, a % 2
-    there = (dy * 4 + dz) * 8 + dx * 2 + s if axis == 0 else (dx * 4 + dz) * 8 + dy * 2 + s
+    there = (dy * 4 + dz) * 8 + dx * 2 + s if axis == 0 else (dz * 4 + dx) * 8 + dy * 2 + s
     return jnp.where(there == b, 1.0, 0.0).astype(BF)
 
 
 def kernel(
     q_ref, k_ref, v_ref, rows_ref, ids_ref, weight_ref, gate_ref, up_ref, down_ref,
-    att_ref, mix_ref, recv_a, recv_b, recv_c, came_a, came_b, came_c,
+    att_ref, mix_ref, recv_a, recv_b, recv_c, came_a, came_b, came_c, mid_a, mid_b, mid_c,
     line_a, line_b, line_c, pack_a, pack_b, pack_c, ids_here, weights_here, info, meta, late_hot,
     kv, queries, v_turned, heads_out, work, gate, up, down, hidden, land, mixing, sum_a, sum_b, sum_c, own_sum,
     send_sem, recv_sem, line_send, line_recv, meta_send, meta_recv, in_send, in_recv,
     kv_send, kv_recv, core_send, core_recv, out_send, out_recv, local_sem,
     load_sem, w_sem, back_send, back_recv, sum_send, sum_recv, land_sem,
+    hop_send, hop_recv, stay_sem,
 ):
     x, y, z, c = place()
     ctx = y * 4 + x
     lines, packs, recvs = (line_a, line_b, line_c), (pack_a, pack_b, pack_c), (recv_a, recv_b, recv_c)
-    cames, sums = (came_a, came_b, came_c), (sum_a, sum_b, sum_c)
+    cames, sums, mids = (came_a, came_b, came_c), (sum_a, sum_b, sum_c), (mid_a, mid_b, mid_c)
     greet_all()
     small = [
         pltpu.make_async_copy(ids_ref, ids_here, land_sem.at[0]),
@@ -149,6 +152,19 @@
     info[8:16, :] = weights_here[...]
     await_all()
 
+    first = []
+    for dz in range(4):
+        zt = (z + dz) % 4
+        for n, ref in enumerate((k_ref, v_ref)):
+            there = ref.at[:, pl.ds(zt * 128, 128)]
+            here = kv.at[ctx, z, c, :, pl.ds(128 * n, 128)]
+            if dz == 0:
+                first.append(pltpu.make_async_copy(there, here, local_sem.at[n]))
+            else:
+                i = (dz - 1) * 3 + n
+                first.append(remote(there, here, in_send.at[i], in_recv.at[i], device(x, y, zt, c)))
+            first[-1].start()
+
     along = {}
     for n, m in enumerate(STEPS):
         for axis, at, width in PARTS:
@@ -163,28 +179,27 @@
             data.start()
             along[axis, m] = (told, data)
 
-    first = []
-    for dz in range(1, 4):
+    asked = []
+    for dz in range(4):
         zt = (z + dz) % 4
-        target = device(x, y, zt, c)
-        for n, (src, dst) in enumerate(
-            (
-                (k_ref.at[:, pl.ds(zt * 128, 128)], kv.at[ctx, z, c, :, pl.ds(0, 128)]),
-                (v_ref.at[:, pl.ds(zt * 128, 128)], kv.at[ctx, z, c, :, pl.ds(128, 128)]),
-                (q_ref.at[:, pl.ds(zt * 1024, 1024)], queries.at[z]),
-            )
-        ):
-            i = (dz - 1) * 3 + n
-            first.append(remote(src, dst, in_send.at[i], in_recv.at[i], target))
-            first[-1].start()
-    own = (
-        (k_ref.at[:, pl.ds(z * 128, 128)], kv.at[ctx, z, c, :, pl.ds(0, 128)]),
-        (v_ref.at[:, pl.ds(z * 128, 128)], kv.at[ctx, z, c, :, pl.ds(128, 128)]),
-        (q_ref.at[:, pl.ds(z * 1024, 1024)], queries.at[z]),
-    )
-    for i, (src, dst) in enumerate(own):
-        first.append(pltpu.make_async_copy(src, dst, local_sem.at[i]))
-        first[-1].start()
+        there = q_ref.at[:, pl.ds(zt * 1024, 1024)]
+        if dz == 0:
+            asked.append(pltpu.make_async_copy(there, queries.at[z], local_sem.at[2]))
+        else:
+            i = (dz - 1) * 3 + 2
+            asked.append(remote(there, queries.at[z], in_send.at[i], in_recv.at[i], device(x, y, zt, c)))
+        asked[-1].start()
+
+    for copy in first:
+        copy.wait()
+    for k in range(1, 16):
+
+        @pl.when(ctx + k < 16)
+        def _():
+            there = ctx + k
+            remote(
+                kv.at[ctx, :, c], kv.at[ctx, :, c], kv_send.at[k - 1], kv_recv.at[k - 1], (there, z * 2 + c)
+            ).start()
 
     weights = [
         pltpu.make_async_copy(gate_ref.at[0], gate, w_sem.at[0]),
@@ -208,38 +223,48 @@
             packs[axis][m] = jnp.dot(
                 hot, lines[axis][TOKENS * m : TOKENS * (m + 1), :], preferred_element_type=F32
             ).astype(BF)
-    for copy in first:
-        copy.wait()
-    for k in range(1, 16):
-
-        @pl.when(ctx + k < 16)
-        def _():
-            there = ctx + k
-            remote(
-                kv.at[ctx, :, c], kv.at[ctx, :, c], kv_send.at[k - 1], kv_recv.at[k - 1], (there, z * 2 + c)
-            ).start()
-
     for axis, at, width in PARTS:
         packs[axis][4] = jnp.dot(late_hot[axis], lines[axis][...], preferred_element_type=F32).astype(BF)
 
+    hops = {}
     sends = ([], [])
     stays = []
-    for core in range(2):
-        for axis, i in shuffled(core):
-            cut = pl.ds(8 * i, 8)
-            n = 31 * axis + i - 1
-            sends[core].append(
-                remote(
-                    packs[axis].at[:, cut], recvs[axis].at[:, cut],
-                    send_sem.at[n], recv_sem.at[n], moved(plane_offset(axis, i)),
+
+    def hop(core):
+        for d1 in STEPS:
+            for axis in range(3):
+                n = (axis * 2 + core) * 3 + d1 - 1
+                hops[axis, core, d1] = remote(
+                    packs[axis].at[:, pl.ds(8 * (16 * core + 4 * d1), 32)], mids[axis].at[core, d1 - 1],
+                    hop_send.at[n], hop_recv.at[n], moved(line_offset((axis + 1) % 3, d1)),
                 )
-            )
-            sends[core][-1].start()
-    for axis in range(3):
-        cut = pl.ds(0, 8)
-        stays.append(pltpu.make_async_copy(packs[axis].at[:, cut], recvs[axis].at[:, cut], local_sem.at[3 + axis]))
-        stays[-1].start()
-
+                hops[axis, core, d1].start()
+
+    def leg(core, d1):
+        for axis in range(3):
+            if d1 > 0:
+                hops[axis, core, d1].wait_recv()
+            for d2 in STEPS + (0,):
+                i = 16 * core + 4 * d1 + d2
+                n = 31 * axis + i - 1
+                here = pl.ds(8 * i, 8)
+                from_ref = packs[axis].at[:, here] if d1 == 0 else mids[axis].at[core, d1 - 1, :, pl.ds(8 * d2, 8)]
+                if core == 0 and d2 == 0:
+                    stays.append(pltpu.make_async_copy(from_ref, recvs[axis].at[:, here], stay_sem.at[4 * axis + d1]))
+                    stays[-1].start()
+                else:
+                    target = moved(line_offset((axis + 2) % 3, d2)[:3] + (core,))
+                    sends[core].append(
+                        remote(from_ref, recvs[axis].at[:, here], send_sem.at[n], recv_sem.at[n], target)
+                    )
+                    sends[core][-1].start()
+
+    hop(0)
+    leg(0, 0)
+    hop(1)
+
+    for copy in asked:
+        copy.wait()
     for k in range(1, 16):
         copy = remote(
             kv.at[ctx, :, c], kv.at[ctx, :, c], kv_send.at[k - 1], kv_recv.at[k - 1], (ctx, z * 2 + c)
@@ -307,19 +332,13 @@
         heads_out[:, :, cut] = result.reshape(4, 64, 128).astype(BF)
         return carry
 
-    lax.fori_loop(0, 8, head, 0)
-    last = []
-    for dz in range(1, 4):
-        zt = (z + dz) % 4
-        last.append(
-            remote(
-                heads_out.at[zt], att_ref.at[:, pl.ds(z * 1024, 1024)],
-                out_send.at[dz - 1], out_recv.at[dz - 1], device(x, y, zt, c),
-            )
-        )
-        last[-1].start()
-    last.append(pltpu.make_async_copy(heads_out.at[z], att_ref.at[:, pl.ds(z * 1024, 1024)], local_sem.at[6]))
-    last[-1].start()
+    for h, d1 in enumerate(STEPS):
+        lax.fori_loop(h, h + 1, head, 0)
+        leg(0, d1)
+    leg(1, 0)
+    lax.fori_loop(3, 4, head, 0)
+    for d1 in STEPS:
+        leg(1, d1)
 
     def load(core):
         at = 128 * core
@@ -328,13 +347,14 @@
                 recv_a.at[dx, pl.ds(at, 128)], work.at[pl.ds(128 * dx, 128), 0:1536], load_sem.at[0]
             ).start()
         pltpu.make_async_copy(recv_a.at[4, pl.ds(at, 128)], work.at[pl.ds(512, 128), 0:1536], load_sem.at[0]).start()
-        for n in range(16):
+        pltpu.make_async_copy(recv_b.at[4, pl.ds(at, 128)], work.at[pl.ds(512, 128), 1536:2816], load_sem.at[0]).start()
+
+        def piece(n, carry):
             pltpu.make_async_copy(
-                recv_b.at[n % 4, pl.ds(at + n // 4 * 32, 32)], work.at[pl.ds(32 * n, 32), 1536:2816], load_sem.at[0]
+                recv_b.at[n // 4 % 4, pl.ds(pl.multiple_of(at + (n % 4 * 4 + n // 16) * 8, 8), 8)],
+                work.at[pl.ds(pl.multiple_of(8 * n, 8), 8), 1536:2816],
+                load_sem.at[0],
             ).start()
-        pltpu.make_async_copy(recv_b.at[4, pl.ds(at, 128)], work.at[pl.ds(512, 128), 1536:2816], load_sem.at[0]).start()
-
-        def piece(n, carry):
             pltpu.make_async_copy(
                 recv_c.at[n % 4, pl.ds(pl.multiple_of(at + n // 4 * 8, 8), 8)],
                 work.at[pl.ds(pl.multiple_of(8 * n, 8), 8), 2816:4096],
@@ -372,7 +392,7 @@
         lax.fori_loop(0, 3, inner, 0)
         if core == 0:
             weights[2].wait()
-        for copy in sends[core]:
+        for copy in [hops[axis, core, d1] for axis in range(3) for d1 in STEPS] + sends[core]:
             copy.wait_send()
         for axis, at, width in PARTS:
             ref = packs[axis]
@@ -386,9 +406,9 @@
                     for dx in range(4):
                         ref[dx, row : row + 128, cut] = value[128 * dx : 128 * (dx + 1)].astype(BF)
                 elif axis == 1:
-                    for n2 in range(16):
-                        to = row + n2 // 4 * 32
-                        ref[n2 % 4, to : to + 32, cut] = value[32 * n2 : 32 * (n2 + 1)].astype(BF)
+                    for n2 in range(64):
+                        to = row + (n2 % 4 * 4 + n2 // 16) * 8
+                        ref[n2 // 4 % 4, to : to + 8, cut] = value[8 * n2 : 8 * (n2 + 1)].astype(BF)
                 else:
                     for n2 in range(64):
                         to = row + n2 // 4 * 8
@@ -432,10 +452,26 @@
                 high = turned.astype(BF)
                 mixing[axis, m, 0:TOKENS, 256 * n : 256 * (n + 1)] = high
                 mixing[axis, m, TOKENS : 2 * TOKENS, 256 * n : 256 * (n + 1)] = (turned - high.astype(F32)).astype(BF)
+    lax.fori_loop(4, 8, head, 0)
+    last = []
+    for dz in range(1, 4):
+        zt = (z + dz) % 4
+        last.append(
+            remote(
+                heads_out.at[zt], att_ref.at[:, pl.ds(z * 1024, 1024)],
+                out_send.at[dz - 1], out_recv.at[dz - 1], device(x, y, zt, c),
+            )
+        )
+        last[-1].start()
+    last.append(pltpu.make_async_copy(heads_out.at[z], att_ref.at[:, pl.ds(z * 1024, 1024)], local_sem.at[6]))
+    last[-1].start()
     for copy in returns:
         copy.wait()
 
-    tiles = [(axis, n) for axis, at, width in PARTS for n in range(width // 256)]
+    groups = [(axis, n) for n in (0, 3) for axis in range(3)]
+    tiles = [
+        (axis, n) for axis, first_tile in groups for n in range(first_tile, min(first_tile + 3, PARTS[axis][2] // 256))
+    ]
 
     def fetch(t):
         axis, n = tiles[t]
@@ -459,13 +495,14 @@
                 own_sum[:, at : at + 256] = total
             else:
                 lines[axis][TOKENS * m : TOKENS * (m + 1), cut] = total.astype(BF)
-        if n == PARTS[axis][2] // 256 - 1:
+        if n in (2, PARTS[axis][2] // 256 - 1):
+            half = slice(0, 768) if n == 2 else slice(768, PARTS[axis][2])
             for s, m in enumerate(STEPS):
-                i = 3 * s + axis
+                i = 3 * s + axis + (9 if n > 2 else 0)
                 parts.append(
                     remote(
-                        lines[axis].at[pl.ds(TOKENS * m, TOKENS)], sums[axis].at[s], sum_send.at[i], sum_recv.at[i],
-                        moved_back(line_offset(axis, m)),
+                        lines[axis].at[pl.ds(TOKENS * m, TOKENS), half], sums[axis].at[s, :, half],
+                        sum_send.at[i], sum_recv.at[i], moved_back(line_offset(axis, m)),
                     )
                 )
                 parts[-1].start()
@@ -492,9 +529,10 @@
     results = pl.pallas_call(
         kernel,
         out_shape=(jax.ShapeDtypeStruct((SEQ, D), BF), jax.ShapeDtypeStruct((TOKENS, D), BF))
-        + tuple(jax.ShapeDtypeStruct((5, 256, w), BF) for w in widths) * 2,
+        + tuple(jax.ShapeDtypeStruct((5, 256, w), BF) for w in widths) * 2
+        + tuple(jax.ShapeDtypeStruct((2, 3, 5, 32, w), BF) for w in widths),
         in_specs=[hbm] * 9,
-        out_specs=(hbm,) * 8,
+        out_specs=(hbm,) * 11,
         scratch_shapes=[pltpu.VMEM((4 * TOKENS, w), BF) for w in widths]
         + [pltpu.VMEM((5, 256, w), BF) for w in widths]
         + [
@@ -518,7 +556,7 @@
         + [pltpu.VMEM((3, TOKENS, w), BF) for w in widths]
         + [pltpu.VMEM((TOKENS, D), F32)]
         + [dma((n,)) for n in (93, 93, 9, 9, 9, 9, 9, 9, 15, 15, 16, 16, 3, 3, 10)]
-        + [dma((n,)) for n in (1, 3, 93, 93, 9, 9, 2)],
+        + [dma((n,)) for n in (1, 3, 93, 93, 18, 18, 2, 18, 18, 12)],
         compiler_params=pltpu.CompilerParams(
             collective_id=0, has_side_effects=True, vmem_limit_bytes=62 * 2**20
         ),

time: 286 us -> 255 us (0.89); the launches traced: 281 us -> 254 us
  Pallas kernels: 276 us -> 249 us
    pallas_call x1, Pallas kernels: 276 us -> 249 us  [body(): pl.pallas_call(kernel, out_shape=(jax.ShapeDtypeStruct((SEQ, D), BF), jax...]
where the time goes in v3:
time: 255 us; the launch traced here: 254 us
  Pallas kernels  249 us (98%)
  local copies, waits for them, and re-layouts  4.16 us (2%)
    pallas_call x1, Pallas kernels, body(): pl.pallas_call(kernel, out_shape=(jax.ShapeDtypeStruct((SEQ, D), BF), jax...  249 us

profile of v3, /device:TPU:1, one launch (start us, length us, event | category | flops | bytes accessed | tf_op | source)
XLA Modules:
  0.0 254.1 jit_solution(1456739634978947618)
XLA Ops:
  0.6 249.3 %attend_and_mix.1 = (bf16[64,4096]{1,0:T(8,128)(2,1)}, bf16[128,4096]{1,0:T(8,128)(2,1)}, bf16[5,256,1536]{2,1,0:T(8,128)(2,1)}, bf16[5,256,1280]{2,1,0:T(8,128)...) custom-call(bf16[64,4096]{1,0:T(8,128)(2,1)} %q_ref.1, ...), custom_call_target="tpu_custom_call" | custom-call | tf_op jit(solution)/shard_map/attend_and_mix/pallas_call | solution.py:529
  250.0 1.9 copy.13
  251.9 2.3 copy.14

commit v4 on v3

--- a/solution.py
+++ b/solution.py
@@ -32,12 +32,6 @@
     return tuple(d)
 
 
-def shuffled(core):
-    order = [(p, i) for p in range(3) for i in range(16 * core, 16 * core + 16)]
-    np.random.RandomState(3 + core).shuffle(order)
-    return [(int(p), int(i)) for p, i in order if i > 0]
-
-
 PEERS = sorted({plane_offset(p, i) for p in range(3) for i in range(1, 32)})
 
 
@@ -122,17 +116,19 @@
 def kernel(
     q_ref, k_ref, v_ref, rows_ref, ids_ref, weight_ref, gate_ref, up_ref, down_ref,
     att_ref, mix_ref, recv_a, recv_b, recv_c, came_a, came_b, came_c, mid_a, mid_b, mid_c,
+    back_mid_a, back_mid_b, back_mid_c,
     line_a, line_b, line_c, pack_a, pack_b, pack_c, ids_here, weights_here, info, meta, late_hot,
     kv, queries, v_turned, heads_out, work, gate, up, down, hidden, land, mixing, sum_a, sum_b, sum_c, own_sum,
     send_sem, recv_sem, line_send, line_recv, meta_send, meta_recv, in_send, in_recv,
     kv_send, kv_recv, core_send, core_recv, out_send, out_recv, local_sem,
     load_sem, w_sem, back_send, back_recv, sum_send, sum_recv, land_sem,
-    hop_send, hop_recv, stay_sem,
+    hop_send, hop_recv, stay_sem, back_hop_send, back_hop_recv,
 ):
     x, y, z, c = place()
     ctx = y * 4 + x
     lines, packs, recvs = (line_a, line_b, line_c), (pack_a, pack_b, pack_c), (recv_a, recv_b, recv_c)
     cames, sums, mids = (came_a, came_b, came_c), (sum_a, sum_b, sum_c), (mid_a, mid_b, mid_c)
+    back_mids = (back_mid_a, back_mid_b, back_mid_c)
     greet_all()
     small = [
         pltpu.make_async_copy(ids_ref, ids_here, land_sem.at[0]),
@@ -336,7 +332,7 @@
         lax.fori_loop(h, h + 1, head, 0)
         leg(0, d1)
     leg(1, 0)
-    lax.fori_loop(3, 4, head, 0)
+    lax.fori_loop(3, 5, head, 0)
     for d1 in STEPS:
         leg(1, d1)
 
@@ -365,7 +361,46 @@
         lax.fori_loop(0, 64, piece, 0)
         pltpu.make_async_copy(recv_c.at[4, pl.ds(at, 128)], work.at[pl.ds(512, 128), 2816:4096], load_sem.at[0]).start()
 
-    returns = []
+    legs = {}
+    back_hops = []
+
+    def back_leg(core):
+        for d1 in STEPS + (0,):
+            for d2 in STEPS + (0,):
+                for axis in range(3):
+                    i = 16 * core + 4 * d1 + d2
+                    n = 31 * axis + i - 1
+                    here = packs[axis].at[:, pl.ds(8 * i, 8)]
+                    there = (
+                        cames[axis].at[:, pl.ds(8 * i, 8)]
+                        if d1 == 0
+                        else back_mids[axis].at[core, d1 - 1, :, pl.ds(8 * d2, 8)]
+                    )
+                    if core == 0 and d2 == 0:
+                        copy = pltpu.make_async_copy(here, there, stay_sem.at[4 * axis + d1])
+                    else:
+                        target = moved_back(line_offset((axis + 2) % 3, d2)[:3] + (core,))
+                        copy = remote(here, there, back_send.at[n], back_recv.at[n], target)
+                    copy.start()
+                    legs[axis, core, d1, d2] = copy
+
+    def back_hop(core, d1):
+        for axis in range(3):
+            for d2 in range(4):
+                copy = legs[axis, core, d1, d2]
+                if core == 0 and d2 == 0:
+                    copy.wait()
+                else:
+                    copy.wait_recv()
+            n = (axis * 2 + core) * 3 + d1 - 1
+            back_hops.append(
+                remote(
+                    back_mids[axis].at[core, d1 - 1], cames[axis].at[:, pl.ds(8 * (16 * core + 4 * d1), 32)],
+                    back_hop_send.at[n], back_hop_recv.at[n], moved_back(line_offset((axis + 1) % 3, d1)),
+                )
+            )
+            back_hops[-1].start()
+
     for core in range(2):
         for copy in sends[core]:
             copy.wait_recv()
@@ -390,6 +425,9 @@
             return carry
 
         lax.fori_loop(0, 3, inner, 0)
+        if core == 1:
+            for d1 in STEPS:
+                back_hop(0, d1)
         if core == 0:
             weights[2].wait()
         for copy in [hops[axis, core, d1] for axis in range(3) for d1 in STEPS] + sends[core]:
@@ -420,23 +458,7 @@
                 return carry
 
             lax.fori_loop(0, width // 256, outer, 0)
-        for axis, i in shuffled(core):
-            cut = pl.ds(8 * i, 8)
-            n = 31 * axis + i - 1
-            returns.append(
-                remote(
-                    packs[axis].at[:, cut], cames[axis].at[:, cut],
-                    back_send.at[n], back_recv.at[n], moved_back(plane_offset(axis, i)),
-                )
-            )
-            returns[-1].start()
-        if core == 0:
-            for axis in range(3):
-                cut = pl.ds(0, 8)
-                returns.append(
-                    pltpu.make_async_copy(packs[axis].at[:, cut], cames[axis].at[:, cut], local_sem.at[3 + axis])
-                )
-                returns[-1].start()
+        back_leg(core)
 
     for axis, at, width in PARTS:
         for m in range(4):
@@ -452,7 +474,10 @@
                 high = turned.astype(BF)
                 mixing[axis, m, 0:TOKENS, 256 * n : 256 * (n + 1)] = high
                 mixing[axis, m, TOKENS : 2 * TOKENS, 256 * n : 256 * (n + 1)] = (turned - high.astype(F32)).astype(BF)
-    lax.fori_loop(4, 8, head, 0)
+    lax.fori_loop(5, 7, head, 0)
+    for d1 in STEPS:
+        back_hop(1, d1)
+    lax.fori_loop(7, 8, head, 0)
     last = []
     for dz in range(1, 4):
         zt = (z + dz) % 4
@@ -465,7 +490,15 @@
         last[-1].start()
     last.append(pltpu.make_async_copy(heads_out.at[z], att_ref.at[:, pl.ds(z * 1024, 1024)], local_sem.at[6]))
     last[-1].start()
-    for copy in returns:
+    for (axis, core, d1, d2), copy in legs.items():
+        if core == 0 and d2 == 0:
+            if d1 == 0:
+                copy.wait()
+        else:
+            copy.wait_send()
+            if d1 == 0:
+                copy.wait_recv()
+    for copy in back_hops:
         copy.wait()
 
     groups = [(axis, n) for n in (0, 3) for axis in range(3)]
@@ -530,9 +563,9 @@
         kernel,
         out_shape=(jax.ShapeDtypeStruct((SEQ, D), BF), jax.ShapeDtypeStruct((TOKENS, D), BF))
         + tuple(jax.ShapeDtypeStruct((5, 256, w), BF) for w in widths) * 2
-        + tuple(jax.ShapeDtypeStruct((2, 3, 5, 32, w), BF) for w in widths),
+        + tuple(jax.ShapeDtypeStruct((2, 3, 5, 32, w), BF) for w in widths) * 2,
         in_specs=[hbm] * 9,
-        out_specs=(hbm,) * 11,
+        out_specs=(hbm,) * 14,
         scratch_shapes=[pltpu.VMEM((4 * TOKENS, w), BF) for w in widths]
         + [pltpu.VMEM((5, 256, w), BF) for w in widths]
         + [
@@ -556,7 +589,7 @@
         + [pltpu.VMEM((3, TOKENS, w), BF) for w in widths]
         + [pltpu.VMEM((TOKENS, D), F32)]
         + [dma((n,)) for n in (93, 93, 9, 9, 9, 9, 9, 9, 15, 15, 16, 16, 3, 3, 10)]
-        + [dma((n,)) for n in (1, 3, 93, 93, 18, 18, 2, 18, 18, 12)],
+        + [dma((n,)) for n in (1, 3, 93, 93, 18, 18, 2, 18, 18, 12, 18, 18)],
         compiler_params=pltpu.CompilerParams(
             collective_id=0, has_side_effects=True, vmem_limit_bytes=62 * 2**20
         ),

time: 255 us -> 249 us (0.976)
  Pallas kernels: 249 us -> 244 us
    pallas_call x1, Pallas kernels: 249 us -> 244 us  [body(): pl.pallas_call(kernel, out_shape=(jax.ShapeDtypeStruct((SEQ, D), BF), jax...]
where the time goes in v4:
time: 249 us
  Pallas kernels  244 us (98%)
  local copies, waits for them, and re-layouts  4.16 us (2%)
    pallas_call x1, Pallas kernels, body(): pl.pallas_call(kernel, out_shape=(jax.ShapeDtypeStruct((SEQ, D), BF), jax...  244 us

profile of v4, /device:TPU:1, one launch (start us, length us, event | category | flops | bytes accessed | tf_op | source)
XLA Modules:
  0.0 248.6 jit_solution(12223959734161283846)
XLA Ops:
  0.6 243.8 %attend_and_mix.1 = (bf16[64,4096]{1,0:T(8,128)(2,1)}, bf16[128,4096]{1,0:T(8,128)(2,1)}, bf16[5,256,1536]{2,1,0:T(8,128)(2,1)}, bf16[5,256,1280]{2,1,0:T(8,128)...) custom-call(bf16[64,4096]{1,0:T(8,128)(2,1)} %q_ref.1, ...), custom_call_target="tpu_custom_call" | custom-call | tf_op jit(solution)/shard_map/attend_and_mix/pallas_call | solution.py:562
  244.4 1.9 copy.13
  246.3 2.3 copy.14

commit v5 on v4

--- a/solution.py
+++ b/solution.py
@@ -246,14 +246,14 @@
                 here = pl.ds(8 * i, 8)
                 from_ref = packs[axis].at[:, here] if d1 == 0 else mids[axis].at[core, d1 - 1, :, pl.ds(8 * d2, 8)]
                 if core == 0 and d2 == 0:
-                    stays.append(pltpu.make_async_copy(from_ref, recvs[axis].at[:, here], stay_sem.at[4 * axis + d1]))
-                    stays[-1].start()
+                    copy = pltpu.make_async_copy(from_ref, recvs[axis].at[:, here], stay_sem.at[4 * axis + d1])
+                    copy.start()
+                    stays.append((axis, copy))
                 else:
                     target = moved(line_offset((axis + 2) % 3, d2)[:3] + (core,))
-                    sends[core].append(
-                        remote(from_ref, recvs[axis].at[:, here], send_sem.at[n], recv_sem.at[n], target)
-                    )
-                    sends[core][-1].start()
+                    copy = remote(from_ref, recvs[axis].at[:, here], send_sem.at[n], recv_sem.at[n], target)
+                    copy.start()
+                    sends[core].append((axis, copy))
 
     hop(0)
     leg(0, 0)
@@ -336,53 +336,53 @@
     for d1 in STEPS:
         leg(1, d1)
 
-    def load(core):
+    def load(core, axis):
         at = 128 * core
-        for dx in range(4):
-            pltpu.make_async_copy(
-                recv_a.at[dx, pl.ds(at, 128)], work.at[pl.ds(128 * dx, 128), 0:1536], load_sem.at[0]
-            ).start()
-        pltpu.make_async_copy(recv_a.at[4, pl.ds(at, 128)], work.at[pl.ds(512, 128), 0:1536], load_sem.at[0]).start()
-        pltpu.make_async_copy(recv_b.at[4, pl.ds(at, 128)], work.at[pl.ds(512, 128), 1536:2816], load_sem.at[0]).start()
-
-        def piece(n, carry):
-            pltpu.make_async_copy(
-                recv_b.at[n // 4 % 4, pl.ds(pl.multiple_of(at + (n % 4 * 4 + n // 16) * 8, 8), 8)],
-                work.at[pl.ds(pl.multiple_of(8 * n, 8), 8), 1536:2816],
-                load_sem.at[0],
-            ).start()
-            pltpu.make_async_copy(
-                recv_c.at[n % 4, pl.ds(pl.multiple_of(at + n // 4 * 8, 8), 8)],
-                work.at[pl.ds(pl.multiple_of(8 * n, 8), 8), 2816:4096],
-                load_sem.at[0],
-            ).start()
-            return carry
-
-        lax.fori_loop(0, 64, piece, 0)
-        pltpu.make_async_copy(recv_c.at[4, pl.ds(at, 128)], work.at[pl.ds(512, 128), 2816:4096], load_sem.at[0]).start()
+        _, left, width = PARTS[axis]
+        columns = pl.ds(left, width)
+        if axis == 0:
+            for dx in range(4):
+                pltpu.make_async_copy(
+                    recv_a.at[dx, pl.ds(at, 128)], work.at[pl.ds(128 * dx, 128), columns], load_sem.at[0]
+                ).start()
+        else:
+
+            def piece(n, carry):
+                dx, dy, dz = n // 16, n // 4 % 4, n % 4
+                m, block = (dy, dz * 4 + dx) if axis == 1 else (dz, dx * 4 + dy)
+                pltpu.make_async_copy(
+                    recvs[axis].at[m, pl.ds(pl.multiple_of(at + block * 8, 8), 8)],
+                    work.at[pl.ds(pl.multiple_of(8 * n, 8), 8), columns],
+                    load_sem.at[0],
+                ).start()
+                return carry
+
+            lax.fori_loop(0, 64, piece, 0)
+        pltpu.make_async_copy(
+            recvs[axis].at[4, pl.ds(at, 128)], work.at[pl.ds(512, 128), columns], load_sem.at[0]
+        ).start()
 
     legs = {}
     back_hops = []
 
-    def back_leg(core):
+    def back_leg(core, axis):
         for d1 in STEPS + (0,):
             for d2 in STEPS + (0,):
-                for axis in range(3):
-                    i = 16 * core + 4 * d1 + d2
-                    n = 31 * axis + i - 1
-                    here = packs[axis].at[:, pl.ds(8 * i, 8)]
-                    there = (
-                        cames[axis].at[:, pl.ds(8 * i, 8)]
-                        if d1 == 0
-                        else back_mids[axis].at[core, d1 - 1, :, pl.ds(8 * d2, 8)]
-                    )
-                    if core == 0 and d2 == 0:
-                        copy = pltpu.make_async_copy(here, there, stay_sem.at[4 * axis + d1])
-                    else:
-                        target = moved_back(line_offset((axis + 2) % 3, d2)[:3] + (core,))
-                        copy = remote(here, there, back_send.at[n], back_recv.at[n], target)
-                    copy.start()
-                    legs[axis, core, d1, d2] = copy
+                i = 16 * core + 4 * d1 + d2
+                n = 31 * axis + i - 1
+                here = packs[axis].at[:, pl.ds(8 * i, 8)]
+                there = (
+                    cames[axis].at[:, pl.ds(8 * i, 8)]
+                    if d1 == 0
+                    else back_mids[axis].at[core, d1 - 1, :, pl.ds(8 * d2, 8)]
+                )
+                if core == 0 and d2 == 0:
+                    copy = pltpu.make_async_copy(here, there, stay_sem.at[4 * axis + d1])
+                else:
+                    target = moved_back(line_offset((axis + 2) % 3, d2)[:3] + (core,))
+                    copy = remote(here, there, back_send.at[n], back_recv.at[n], target)
+                copy.start()
+                legs[axis, core, d1, d2] = copy
 
     def back_hop(core, d1):
         for axis in range(3):
@@ -402,12 +402,15 @@
             back_hops[-1].start()
 
     for core in range(2):
-        for copy in sends[core]:
-            copy.wait_recv()
-        if core == 0:
-            for copy in stays:
-                copy.wait()
-        load(core)
+        for axis in range(3):
+            for part, copy in sends[core]:
+                if part == axis:
+                    copy.wait_recv()
+            if core == 0:
+                for part, copy in stays:
+                    if part == axis:
+                        copy.wait()
+            load(core, axis)
         pltpu.make_async_copy(work, work, load_sem.at[0]).wait()
         if core == 0:
             weights[0].wait()
@@ -430,7 +433,7 @@
                 back_hop(0, d1)
         if core == 0:
             weights[2].wait()
-        for copy in [hops[axis, core, d1] for axis in range(3) for d1 in STEPS] + sends[core]:
+        for copy in [hops[axis, core, d1] for axis in range(3) for d1 in STEPS] + [copy for _, copy in sends[core]]:
             copy.wait_send()
         for axis, at, width in PARTS:
             ref = packs[axis]
@@ -458,8 +461,7 @@
                 return carry
 
             lax.fori_loop(0, width // 256, outer, 0)
-        back_leg(core)
-
+            back_leg(core, axis)
     for axis, at, width in PARTS:
         for m in range(4):
             early, late = slot_masks(ranks(meta[axis, m], owners(axis)), m)

time: 249 us -> 246 us (0.988)
  Pallas kernels: 244 us -> 239 us
    pallas_call x1, Pallas kernels: 244 us -> 239 us  [body(): pl.pallas_call(kernel, out_shape=(jax.ShapeDtypeStruct((SEQ, D), BF), jax...]
where the time goes in v5:
time: 246 us; the launch traced here: 244 us
  Pallas kernels  239 us (97%)
  local copies, waits for them, and re-layouts  4.16 us (2%)
    pallas_call x1, Pallas kernels, body(): pl.pallas_call(kernel, out_shape=(jax.ShapeDtypeStruct((SEQ, D), BF), jax...  239 us

profile of v5, /device:TPU:1, one launch (start us, length us, event | category | flops | bytes accessed | tf_op | source)
XLA Modules:
  0.0 244.0 jit_solution(4335120241838074554)
XLA Ops:
  0.6 239.2 %attend_and_mix.1 = (bf16[64,4096]{1,0:T(8,128)(2,1)}, bf16[128,4096]{1,0:T(8,128)(2,1)}, bf16[5,256,1536]{2,1,0:T(8,128)(2,1)}, bf16[5,256,1280]{2,1,0:T(8,128)...) custom-call(bf16[64,4096]{1,0:T(8,128)(2,1)} %q_ref.1, ...), custom_call_target="tpu_custom_call" | custom-call | tf_op jit(solution)/shard_map/attend_and_mix/pallas_call | solution.py:564
  239.8 1.9 copy.13
  241.7 2.3 copy.14
